TPU v7x, 32 devices: a whole 2x2x4 slice. The times are simulated.
32 devices in a mesh: sec: 4 (over x, core), gx: 8 (over z, y).
Axes of the slice: x: 2, y: 2, z: 4, core: 2. Of those that a mesh axis runs over, the one named last changes fastest.
Arguments:
- ocean_state: float32 [4, 4, 96, 256], P(None, None, 'gx'), may hold values from -4 to 4
- heat_first: float32 [4, 96, 256], P(None, 'gx'), may hold values from 0 to 1.5
- wind_stress: float32 [2, 96, 256], P(None, 'gx'), may hold values from -3 to 3
- shortwave: float32 [96, 256], P('gx'), may hold values from 1 to 6
- sea_mask: int32 [96, 256], P('gx'), may hold values from 0 to 1, as said below
- owner_cols: int32 [8, 3, 8, 128], P('gx'), may hold values from -1 to 3071, as said below
- tracers: float32 [19, 4, 32768], P(None, None, ('sec', 'gx')), may hold values from 0.2 to 2
Outputs:
- tracers_out: float32 [19, 4, 32768], P(None, None, ('sec', 'gx'))
- heating_out: float32 [4, 32768], P(None, ('sec', 'gx'))
Inputs may be any that keep to these rules, and one draw needn't show every extreme that they name: `sea_mask`: 1 marks a sea column, 0 land; within a strip, column j is sea wherever j % 128 = 127 and in the last 128 columns. `owner_cols`: entry [g, s, h, j] is slot j of the list of strip g's sea columns owned by the tracer device of section s + 1 and gx index h, strip g being the cells at gx index g; a column is x 256 + y with x counted within the strip, and -1 marks an empty slot. Every sea column of a strip stands in exactly one slot and no land column does; the used slots of a list come first, in ascending order; every list holds at least one column. In every draw one tracer device has full lists from every strip.
All inputs are finite; a program needn't handle non-finite values.
Results may differ from a plain program's by a relative error of at most 0.00002.
Values sent between devices are 32-bit elements; how exact they have to be, the bound alone decides.
A program may use at most 192 MiB of HBM per device.

v0:
```python
import jax
import jax.numpy as jnp
import numpy as np
from jax import lax
from jax.sharding import PartitionSpec as P

STEPS = 2


DT_OCEAN = 0.15
VISCOSITY = 0.2
DIFFUSIVITY = 0.15
DAMPING = 0.05
CORIOLIS = 0.8
HEAT_GAIN = 4.0
ONE_THIRD = 1.0 / 3.0
TWO_THIRDS = 2.0 / 3.0
DT_BIO = 0.8
W_LIMIT = 0.35
W_GAIN = 0.25
KV_BASE = 0.05
KV_SHEAR = 0.3
GAS_RATE = 0.5
WATER_ATTEN = 0.15
CHLORO_ATTEN = 0.1
HEATUP_PER_STEP = 0.5
GROWTH = 0.6
GRAZING = 0.4
REMINERAL = 0.2
EXCRETION = 0.1
PHYTO_LOSS = 0.05
ZOO_LOSS = 0.05
ASSIMILATE = 0.6
YIELDS = np.array(
    [
        0.0,
        0.0,
        0.0,
        0.0,
        -1.3,
        1.0,
        0.16,
        0.9,
        -0.6,
        0.4,
        1.2,
        -0.8,
        0.5,
        0.3,
        -0.4,
        0.7,
        -1.0,
        0.2,
        0.6,
    ],
    np.float32,
)
DECAYS = np.array(
    [
        0.0,
        0.0,
        0.0,
        0.0,
        0.02,
        0.01,
        0.05,
        0.03,
        0.08,
        0.04,
        0.02,
        0.06,
        0.1,
        0.03,
        0.07,
        0.05,
        0.02,
        0.09,
        0.04,
    ],
    np.float32,
)
GAS_ON = np.array([0, 0, 0, 0, 1, 1] + [0] * 13, np.float32)
SOLUBILITY_BASE = np.array([0, 0, 0, 0, 1.2, 1.0] + [0] * 13, np.float32)
SOLUBILITY_HEAT = np.array([0, 0, 0, 0, -0.5, -0.3] + [0] * 13, np.float32)
SOLUBILITY_BRINE = np.array([0, 0, 0, 0, 0.1, 0.3] + [0] * 13, np.float32)


def padded_2(block, sides, width):
    for axis, dim in sides:
        count = lax.axis_size(axis)
        forward = [(i, i + 1) for i in range(count - 1)]
        forward.append((count - 1, 0))
        backward = [(target, source) for source, target in forward]
        low = lax.ppermute(
            lax.slice_in_dim(block, block.shape[dim] - width, None, axis=dim), axis, forward
        )
        high = lax.ppermute(lax.slice_in_dim(block, 0, width, axis=dim), axis, backward)
        block = jnp.concatenate([low, block, high], axis=dim)
    return block


def coriolis_profile(count):
    lat_index = jnp.arange(count, dtype=jnp.float32)
    return CORIOLIS * (2.0 * (lat_index + 0.5) / count - 1.0)


def trimmed(values, margin):
    return values[..., margin : values.shape[-2] - margin, :]


def ocean_rates(
    centre, east_cells, west_cells, north_cells, south_cells, heating, sea_cells, stress, coriolis_y
):
    laplace = east_cells + west_cells + north_cells + south_cells - 4.0 * centre
    along_x = 0.5 * (east_cells - west_cells)
    along_y = 0.5 * (north_cells - south_cells)
    zonal_vel = centre[0]
    meridional = centre[1]
    levels = centre.shape[1]
    top_level = (jnp.arange(levels) == 0).astype(jnp.float32)[:, None, None]
    zonal_rate = (
        coriolis_y * meridional
        - DAMPING * zonal_vel
        + VISCOSITY * laplace[0]
        + top_level * stress[0]
    )
    merid_rate = (
        -coriolis_y * zonal_vel
        - DAMPING * meridional
        + VISCOSITY * laplace[1]
        + top_level * stress[1]
    )
    heat_rate = (
        -(zonal_vel * along_x[2] + meridional * along_y[2])
        + DIFFUSIVITY * laplace[2]
        + HEAT_GAIN * heating
    )
    salt_rate = -(zonal_vel * along_x[3] + meridional * along_y[3]) + DIFFUSIVITY * laplace[3]
    return jnp.stack([zonal_rate, merid_rate, heat_rate, salt_rate]) * sea_cells


def ocean_tendency(padded, heating, sea_cells, stress, coriolis_y):
    centre = padded[:, :, 1:-1]
    edge_zeros = jnp.zeros_like(centre[..., :1])
    north_cells = jnp.concatenate([centre[..., 1:], edge_zeros], axis=-1)
    south_cells = jnp.concatenate([edge_zeros, centre[..., :-1]], axis=-1)
    return ocean_rates(
        centre,
        padded[:, :, 2:],
        padded[:, :, :-2],
        north_cells,
        south_cells,
        heating,
        sea_cells,
        stress,
        coriolis_y,
    )


def column_fields(current, zonal_padded, stress, shortwave):
    meridional = current[1]
    edge_zeros = jnp.zeros_like(meridional[..., :1])
    merid_north = jnp.concatenate([meridional[..., 1:], edge_zeros], axis=-1)
    merid_south = jnp.concatenate([edge_zeros, meridional[..., :-1]], axis=-1)
    divergence = 0.5 * (zonal_padded[:, 2:] - zonal_padded[:, :-2]) + 0.5 * (
        merid_north - merid_south
    )
    return finish_fields(current, divergence, stress, shortwave)


def finish_fields(current, divergence, stress, shortwave):
    zonal_vel = current[0]
    meridional = current[1]
    levels = current.shape[1]
    from_bottom = jnp.cumsum(divergence[::-1], axis=0)[::-1]
    below_top = (jnp.arange(levels) > 0).astype(jnp.float32)[:, None, None]
    upwelling = W_LIMIT * jnp.tanh(W_GAIN * from_bottom) * below_top
    shear_sq = (zonal_vel[1:] - zonal_vel[:-1]) ** 2 + (meridional[1:] - meridional[:-1]) ** 2
    mixing = KV_BASE + KV_SHEAR * shear_sq / (1.0 + shear_sq)
    mixing = jnp.concatenate([jnp.zeros_like(mixing[:1]), mixing], axis=0)
    grid_box_space = jnp.stack([current[2], current[3], upwelling, mixing])
    surface = jnp.stack([stress[0] * stress[0] + stress[1] * stress[1], shortwave])
    return (grid_box_space.reshape(4, levels, -1), surface.reshape(2, -1))


def minmod(one_side, other_side):
    return jnp.maximum(0.0, jnp.minimum(one_side, other_side)) + jnp.minimum(
        0.0, jnp.maximum(one_side, other_side)
    )


def biogeochem(grid_box_space, surface, validity, species_now):
    marine_thermal_state = grid_box_space[0]
    brine_content = grid_box_space[1]
    upwelling = grid_box_space[2]
    mixing = grid_box_space[3]
    wind_power = surface[0]
    sunlight = surface[1]
    level_zero = jnp.zeros_like(species_now[:, :1])
    step_diff = species_now[:, 1:] - species_now[:, :-1]
    slopes = minmod(
        jnp.concatenate([step_diff, level_zero], axis=1),
        jnp.concatenate([level_zero, step_diff], axis=1),
    )
    courant = jnp.abs(upwelling) * DT_BIO
    above_cell = jnp.concatenate([species_now[:, :1], species_now[:, :-1]], axis=1)
    above_slope = jnp.concatenate([slopes[:, :1], slopes[:, :-1]], axis=1)
    from_below = species_now - 0.5 * (1.0 - courant) * slopes
    from_above = above_cell + 0.5 * (1.0 - courant) * above_slope
    updraft_flux = (
        jnp.maximum(upwelling, 0.0) * from_below + jnp.minimum(upwelling, 0.0) * from_above
    )
    advect = jnp.concatenate([updraft_flux[:, 1:], level_zero], axis=1) - updraft_flux
    down_mix = mixing * (above_cell - species_now)
    diffuse = down_mix - jnp.concatenate([down_mix[:, 1:], level_zero], axis=1)
    transported = species_now + DT_BIO * (advect + diffuse)
    transfer = GAS_RATE * wind_power / (1.0 + wind_power)
    dissolved_limit = (
        SOLUBILITY_BASE[:, None]
        + SOLUBILITY_HEAT[:, None] * marine_thermal_state[0]
        + SOLUBILITY_BRINE[:, None] * brine_content[0]
    )
    exchange_top = GAS_ON[:, None] * DT_BIO * transfer * (dissolved_limit - transported[:, 0])
    transported = jnp.concatenate(
        [(transported[:, 0] + exchange_top)[:, None], transported[:, 1:]], axis=1
    )
    nutrient = transported[0]
    phytoplankton = transported[1]
    zooplank = transported[2]
    detritus = transported[3]
    extinction = WATER_ATTEN + CHLORO_ATTEN * jnp.abs(phytoplankton)
    above_ext = jnp.cumsum(extinction, axis=0) - extinction
    top_light = sunlight * jnp.exp(-above_ext)
    mid_light = top_light * jnp.exp(-0.5 * extinction)
    heating = top_light - top_light * jnp.exp(-extinction)
    heatup_increment = jnp.exp(HEATUP_PER_STEP * marine_thermal_state)
    growth = (
        GROWTH
        * heatup_increment
        * mid_light
        / (mid_light + 1.0)
        * jnp.abs(nutrient)
        / (jnp.abs(nutrient) + 1.0)
        * phytoplankton
    )
    grazing = (
        GRAZING
        * heatup_increment
        * phytoplankton
        * phytoplankton
        / (phytoplankton * phytoplankton + 1.0)
        * zooplank
    )
    remineral = REMINERAL * heatup_increment * detritus
    nutrient_rate = -growth + remineral + EXCRETION * zooplank
    phyto_rate = growth - grazing - PHYTO_LOSS * phytoplankton
    zoo_rate = ASSIMILATE * grazing - EXCRETION * zooplank - ZOO_LOSS * zooplank
    detritus_rate = (
        (1.0 - ASSIMILATE) * grazing + PHYTO_LOSS * phytoplankton + ZOO_LOSS * zooplank - remineral
    )
    others = (
        YIELDS[4:, None, None] * (remineral - growth) - DECAYS[4:, None, None] * transported[4:]
    )
    change = jnp.concatenate(
        [jnp.stack([nutrient_rate, phyto_rate, zoo_rate, detritus_rate]), others], axis=0
    )
    reacted = transported + DT_BIO * change
    return (validity * reacted + (1.0 - validity) * species_now, validity * heating)


def per_device(ocean_state, heat_first, wind_stress, shortwave, sea_mask, owner_cols, tracers):
    sec_count = lax.axis_size("sec")
    strip_count = lax.axis_size("gx")
    section = lax.axis_index("sec")
    is_ocean = section == 0
    levels = ocean_state.shape[1]
    strip_width = ocean_state.shape[2]
    lat_count = ocean_state.shape[3]
    strip_cols = strip_width * lat_count
    coriolis_y = coriolis_profile(lat_count)
    sea_cells = sea_mask.astype(jnp.float32)
    slot_lists = owner_cols[0]
    pair_slots = slot_lists.shape[-1]
    peer_count = sec_count * strip_count
    dev_slots = strip_count * pair_slots
    flat_lists = slot_lists.reshape(-1)
    listed = (flat_lists >= 0).astype(jnp.float32)
    list_index = jnp.maximum(flat_lists, 0)

    def on_ocean(compute_it, skip_it, operand):
        return lax.cond(is_ocean, compute_it, skip_it, operand)

    def keep_centre(padded):
        return trimmed(padded, 1)

    def segment_halo(current):
        padded = padded_2(current.reshape(4 * levels, strip_width, lat_count), (("gx", 1),), 1)
        return padded.reshape(4, levels, strip_width + 2, lat_count)

    def zonal_rim(current):
        return padded_2(current[0], (("gx", 1),), 1)

    def forward(current):
        zonal_padded = zonal_rim(current)

        def build(operand):
            grid_box_space, surface = column_fields(operand[0], operand[1], wind_stress, shortwave)
            gap_volume = jnp.zeros((4, levels, dev_slots), jnp.float32)
            gap_surface = jnp.zeros((2, dev_slots), jnp.float32)
            gap_mark = jnp.zeros((dev_slots,), jnp.float32)
            vol_out = jnp.concatenate(
                [gap_volume, jnp.take(grid_box_space, list_index, axis=2) * listed], axis=2
            )
            surf_out = jnp.concatenate(
                [gap_surface, jnp.take(surface, list_index, axis=1) * listed], axis=1
            )
            mark_out = jnp.concatenate([gap_mark, listed])
            return (
                vol_out.reshape(4, levels, peer_count, pair_slots),
                surf_out.reshape(2, 1, peer_count, pair_slots),
                mark_out.reshape(1, 1, peer_count, pair_slots),
            )

        def silent(operand):
            return (
                jnp.zeros((4, levels, peer_count, pair_slots), jnp.float32),
                jnp.zeros((2, 1, peer_count, pair_slots), jnp.float32),
                jnp.zeros((1, 1, peer_count, pair_slots), jnp.float32),
            )

        vol_out, surf_out, mark_out = lax.cond(is_ocean, build, silent, (current, zonal_padded))
        vol_in, surf_in, mark_in = (
            lax.all_to_all(vol_out, ("sec", "gx"), split_axis=2, concat_axis=2, tiled=True),
            lax.all_to_all(surf_out, ("sec", "gx"), split_axis=2, concat_axis=2, tiled=True),
            lax.all_to_all(mark_out, ("sec", "gx"), split_axis=2, concat_axis=2, tiled=True),
        )
        return (
            vol_in[:, :, :strip_count].reshape(4, levels, dev_slots),
            surf_in[:, :, :strip_count].reshape(2, dev_slots),
            mark_in[:, :, :strip_count].reshape(dev_slots),
        )

    def backward(heat_slots):
        blocks = heat_slots.reshape(levels, strip_count, pair_slots)
        filler = jnp.zeros((levels, (sec_count - 1) * strip_count, pair_slots), jnp.float32)
        outgoing = jnp.concatenate([blocks, filler], axis=1)
        returned = lax.all_to_all(outgoing, ("sec", "gx"), split_axis=1, concat_axis=1, tiled=True)
        owned_heat = returned[:, strip_count:].reshape(levels, -1)

        def place_heat(portion):
            placed = jnp.zeros((levels, strip_cols), jnp.float32).at[:, list_index].add(portion)
            return placed.reshape(levels, strip_width, lat_count)

        def no_heat(portion):
            return jnp.zeros((levels, strip_width, lat_count), jnp.float32)

        return lax.cond(is_ocean, place_heat, no_heat, owned_heat)

    current = ocean_state
    heating = heat_first
    species_now = tracers
    heat_slots = jnp.zeros((levels, tracers.shape[-1]), jnp.float32)
    for coupling in range(STEPS):

        def segment_rate(padded):
            return ocean_tendency(padded, heating, sea_cells, wind_stress, coriolis_y)

        def first_rule(padded):
            return trimmed(padded, 1) + DT_OCEAN * segment_rate(padded)

        def second_rule(padded):
            return 0.75 * current + 0.25 * (trimmed(padded, 1) + DT_OCEAN * segment_rate(padded))

        def third_rule(padded):
            return ONE_THIRD * current + TWO_THIRDS * (
                trimmed(padded, 1) + DT_OCEAN * segment_rate(padded)
            )

        segment_one = on_ocean(first_rule, keep_centre, segment_halo(current))
        segment_two = on_ocean(second_rule, keep_centre, segment_halo(segment_one))
        current = on_ocean(third_rule, keep_centre, segment_halo(segment_two))
        incoming = forward(current)

        def tracer_compute_it(operand):
            return biogeochem(operand[0], operand[1], operand[2], operand[3])

        def tracer_skip_it(operand):
            return (operand[3], jnp.zeros((levels, operand[3].shape[-1]), jnp.float32))

        species_now, heat_slots = lax.cond(
            is_ocean,
            tracer_skip_it,
            tracer_compute_it,
            (incoming[0], incoming[1], incoming[2], species_now),
        )
        if coupling + 1 < STEPS:
            heating = backward(heat_slots)
    return (species_now, heat_slots)


def solution(mesh):
    return jax.shard_map(
        per_device,
        mesh=mesh,
        in_specs=(
            P(None, None, "gx", None),
            P(None, "gx", None),
            P(None, "gx", None),
            P("gx", None),
            P("gx", None),
            P("gx", None, None, None),
            P(None, None, ("sec", "gx")),
        ),
        out_specs=(P(None, None, ("sec", "gx")), P(None, ("sec", "gx"))),
        check_vma=False,
    )
```

profile of v0, /device:TPU:1, one launch (start us, length us, event | category | flops | bytes accessed | tf_op | source)
XLA Modules:
  0.0 313.5 jit_solution(859265524221744044)
XLA Ops:
  3.9 3.1 collective-permute-start.1
  8.9 3.7 %collective-permute-start.3 = (f32[16,1,256]{2,1,0:T(1,128)S(1)}, f32[16,1,256]{2,1,0:T(1,128)S(1)}, u32[]{:S(2)}, u32[]{:S(2)}) collective-permute-start(f32[16,1,256]{2,1,0:T(1,128)S(1)} %get-tuple-element.624), channel_id=1, source_target_pairs={{1,0},{2,1},{3,2},{4,3},{5,4},{6,5},{7,6},{0,7},{9,8},{10,9},{11,1... | collective-permute-start | bytes 49160 | tf_op jit(solution)/shard_map/ppermute | solution.py:97
  13.9 4.3 %collective-permute-start.5 = (f32[16,1,256]{2,1,0:T(1,128)S(1)}, f32[16,1,256]{2,1,0:T(1,128)S(1)}, u32[]{:S(2)}, u32[]{:S(2)}) collective-permute-start(f32[16,1,256]{2,1,0:T(1,128)S(1)} %get-tuple-element.622), channel_id=1, source_target_pairs={{1,0},{2,1},{3,2},{4,3},{5,4},{6,5},{7,6},{0,7},{9,8},{10,9},{11,1... | collective-permute-start | bytes 49160 | tf_op jit(solution)/shard_map/ppermute | solution.py:97
  19.4 4.3 %collective-permute-start.9 = (f32[4,1,256]{2,1,0:T(1,128)S(1)}, f32[4,1,256]{2,1,0:T(1,128)S(1)}, u32[]{:S(2)}, u32[]{:S(2)}) collective-permute-start(f32[4,1,256]{2,1,0:T(1,128)S(1)} %get-tuple-element.630), channel_id=1, source_target_pairs={{1,0},{2,1},{3,2},{4,3},{5,4},{6,5},{7,6},{0,7},{9,8},{10,9},{11,1... | collective-permute-start | bytes 12296 | tf_op jit(solution)/shard_map/ppermute | solution.py:97
  24.7 6.1 %conditional.14 = (f32[4,4,32,128]{1,0,3,2:T(4,128)}, f32[2,1,32,128]{0,3,2,1:T(8,128)S(1)}, f32[1,1,32,128]{3,2,1,0:T(8,128)}) conditional(s32[]{:T(128)} %convert_element_type.86, () %tuple.94, (f32[4,4,12,256]{3,2,1,0:T(8,128)S(1)}, f32[4,14,256]{2,1,0:T(8,128)S(1)}, s32[3072]{0:T(1024)S(1)}, f32[3072]{0:T(1024)S(1)}, ...), branch_computations={%region_6.0_spmd, %region_7.11_spmd} | conditional | flops 448520 | bytes 4239300 | solution.py:331
  24.7 5.3 %broadcast.1165 = f32[4,4,32,128]{1,0,3,2:T(4,128)} broadcast(f32[]{:T(128)} %constant.101.clone), dimensions={} | broadcast | bytes 262148 | tf_op jit(solution)/shard_map/broadcast.68
  30.8 75.1 %all-to-all-start = ((f32[1,1,32,128]{3,1,0,2:T(1,128)}), f32[1,1,32,128]{3,1,0,2:T(1,128)S(1)}, u32[]{:S(2)}, u32[]{:S(2)}) async-start(f32[1,1,32,128]{3,1,0,2:T(1,128)} %bitcast.84), calls=%async_computation | async-start | bytes 32768 | tf_op jit(solution)/shard_map/all_to_all | solution.py:335
  107.2 5.4 %all-to-all-done = f32[1,1,32,128]{3,1,0,2:T(1,128)S(1)} async-done(((f32[1,1,32,128]{3,1,0,2:T(1,128)}), f32[1,1,32,128]{3,1,0,2:T(1,128)S(1)}, u32[]{:S(2)}, u32[]{:S(2)}) %all-to-all-start) | async-done | bytes 16416 | tf_op jit(solution)/shard_map/all_to_all | solution.py:335
  115.5 7.4 %copy.98 = f32[4,4,32,128]{3,1,0,2:T(4,128)} copy(f32[4,4,32,128]{1,0,3,2:T(4,128)} %get-tuple-element.314) | data formatting | bytes 524288 | tf_op jit(solution)/shard_map/cond | solution.py:331
  122.9 6.0 %all-to-all-start.1 = ((f32[4,4,32,128]{3,1,0,2:T(4,128)}), f32[4,4,32,128]{3,1,0,2:T(4,128)S(1)}, u32[]{:S(2)}, u32[]{:S(2)}) async-start(f32[4,4,32,128]{3,1,0,2:T(4,128)} %copy.98), calls=%async_computation.1 | async-start | bytes 524288 | tf_op jit(solution)/shard_map/all_to_all | solution.py:333
  130.3 2.8 collective-permute-start.7
  133.2 6.2 %all-to-all-done.1 = f32[4,4,32,128]{3,1,0,2:T(4,128)S(1)} async-done(((f32[4,4,32,128]{3,1,0,2:T(4,128)}), f32[4,4,32,128]{3,1,0,2:T(4,128)S(1)}, u32[]{:S(2)}, u32[]{:S(2)}) %all-to-all-start.1) | async-done | bytes 262176 | tf_op jit(solution)/shard_map/all_to_all | solution.py:333
  139.4 3.3 %conditional.15 = (f32[19,4,1024]{2,1,0:T(4,128)S(1)}, f32[4,1024]{1,0:T(4,128)S(1)}) conditional(s32[]{:T(128)} %convert_element_type.86, (f32[1,1,32,128]{3,1,0,2:T(1,128)S(1)}, f32[4,4,32,128]{3,1,0,2:T(4,128)S(1)}, f32[19,4,1024]{2,1,0:T(4,128)S(1)}, f32[19,1]{0,1:T(1,128)S(1)}, f32[2,1,32,128]{3,1,0,2:T(1,128)S(1)}, ...), branch_computations={%region_9.13_spmd, %region_11.14_spmd} | conditional | flops 3310591 | bytes 12699484 | solution.py:390
  146.1 7.1 %all-to-all-done.3 = f32[4,32,128]{2,0,1:T(4,128)S(1)} async-done(((f32[4,32,128]{2,0,1:T(4,128)}), f32[4,32,128]{2,0,1:T(4,128)S(1)}, u32[]{:S(2)}, u32[]{:S(2)}) %all-to-all-start.3) | async-done | bytes 65568 | tf_op jit(solution)/shard_map/all_to_all | solution.py:347
  154.0 3.7 %collective-permute-start.11 = (f32[16,1,256]{2,1,0:T(1,128)S(1)}, f32[16,1,256]{2,1,0:T(1,128)S(1)}, u32[]{:S(2)}, u32[]{:S(2)}) collective-permute-start(f32[16,1,256]{2,1,0:T(1,128)S(1)} %get-tuple-element.618), channel_id=1, source_target_pairs={{1,0},{2,1},{3,2},{4,3},{5,4},{6,5},{7,6},{0,7},{9,8},{10,9},{11,1... | collective-permute-start | bytes 49160 | tf_op jit(solution)/shard_map/ppermute | solution.py:97
  158.9 4.2 %collective-permute-start.13 = (f32[16,1,256]{2,1,0:T(1,128)S(1)}, f32[16,1,256]{2,1,0:T(1,128)S(1)}, u32[]{:S(2)}, u32[]{:S(2)}) collective-permute-start(f32[16,1,256]{2,1,0:T(1,128)S(1)} %get-tuple-element.616), channel_id=1, source_target_pairs={{1,0},{2,1},{3,2},{4,3},{5,4},{6,5},{7,6},{0,7},{9,8},{10,9},{11,1... | collective-permute-start | bytes 49160 | tf_op jit(solution)/shard_map/ppermute | solution.py:97
  164.4 4.3 %collective-permute-start.15 = (f32[4,1,256]{2,1,0:T(1,128)S(1)}, f32[4,1,256]{2,1,0:T(1,128)S(1)}, u32[]{:S(2)}, u32[]{:S(2)}) collective-permute-start(f32[4,1,256]{2,1,0:T(1,128)S(1)} %get-tuple-element.628), channel_id=1, source_target_pairs={{1,0},{2,1},{3,2},{4,3},{5,4},{6,5},{7,6},{0,7},{9,8},{10,9},{11,1... | collective-permute-start | bytes 12296 | tf_op jit(solution)/shard_map/ppermute | solution.py:97
  169.7 6.1 %conditional.20 = (f32[4,4,32,128]{1,0,3,2:T(4,128)}, f32[2,1,32,128]{0,3,2,1:T(8,128)S(1)}, f32[1,1,32,128]{3,2,1,0:T(8,128)}) conditional(s32[]{:T(128)} %convert_element_type.86, () %tuple.89, (f32[4,4,12,256]{3,2,1,0:T(8,128)S(1)}, f32[4,14,256]{2,1,0:T(8,128)S(1)}, s32[3072]{0:T(1024)S(1)}, f32[3072]{0:T(1024)S(1)}, ...), branch_computations={%region_21.24_spmd, %region_22.26_spmd} | conditional | flops 448520 | bytes 4239300 | solution.py:331
  169.7 5.3 %broadcast.1259 = f32[4,4,32,128]{1,0,3,2:T(4,128)} broadcast(f32[]{:T(128)} %constant.225.clone), dimensions={} | broadcast | bytes 262148 | tf_op jit(solution)/shard_map/broadcast.202
  175.8 100.0 %all-to-all-start.4 = ((f32[1,1,32,128]{3,1,0,2:T(1,128)}), f32[1,1,32,128]{3,1,0,2:T(1,128)S(1)}, u32[]{:S(2)}, u32[]{:S(2)}) async-start(f32[1,1,32,128]{3,1,0,2:T(1,128)} %bitcast.93), calls=%async_computation.4 | async-start | bytes 32768 | tf_op jit(solution)/shard_map/all_to_all | solution.py:335
  277.0 5.4 %all-to-all-done.4 = f32[1,1,32,128]{3,1,0,2:T(1,128)S(1)} async-done(((f32[1,1,32,128]{3,1,0,2:T(1,128)}), f32[1,1,32,128]{3,1,0,2:T(1,128)S(1)}, u32[]{:S(2)}, u32[]{:S(2)}) %all-to-all-start.4) | async-done | bytes 16416 | tf_op jit(solution)/shard_map/all_to_all | solution.py:335
  285.3 6.8 %copy.112 = f32[4,4,32,128]{3,1,0,2:T(4,128)S(1)} copy(f32[4,4,32,128]{1,0,3,2:T(4,128)} %get-tuple-element.318) | data formatting | bytes 524288 | tf_op jit(solution)/shard_map/cond | solution.py:331
  292.4 15.6 %all_to_all.35 = f32[4,4,32,128]{3,1,0,2:T(4,128)S(1)} all-to-all(f32[4,4,32,128]{3,1,0,2:T(4,128)S(1)} %copy.112), channel_id=1, replica_groups=mesh['sec'=4,'gx'=8] {'sec','gx'}, dimensions={2} | all-to-all | bytes 524288 | tf_op jit(solution)/shard_map/all_to_all | solution.py:333
  308.0 5.5 %conditional.21 = (f32[19,4,1024]{2,1,0:T(4,128)}, f32[4,1024]{1,0:T(4,128)}) conditional(s32[]{:T(128)} %convert_element_type.86, (f32[1,1,32,128]{3,1,0,2:T(1,128)S(1)}, f32[4,4,32,128]{3,1,0,2:T(4,128)S(1)}, f32[19,4,1024]{2,1,0:T(4,128)}, f32[19,1]{0,1:T(1,128)S(1)}, f32[2,1,32,128]{3,1,0,2:T(1,128)S(1)}, /*index=5*/f32[19,1]{0,1:T(1,128)S(1)}, ...), branch_computations={%region_24.28_spmd, %region_26.29_spmd} | conditional | flops 3310591 | bytes 15189372 | solution.py:390
  (181 shorter events, 36.2 us)
Async XLA Ops:
  1.8 6.3 %collective-permute-start = (f32[16,1,256]{2,0,1:T(8,128)S(1)}, f32[16,1,256]{2,0,1:T(8,128)S(1)}, u32[]{:S(2)}, u32[]{:S(2)}) collective-permute-start(f32[16,1,256]{2,0,1:T(8,128)S(1)} %get-tuple-element.625), channel_id=1, source_target_pairs={{0,1},{1,2},{2,3},{3,4},{4,5},{5,6},{6,7},{7,0},{8,9},{9,10},{10,1... | collective-permute-start | bytes 49160 | tf_op jit(solution)/shard_map/ppermute | solution.py:94
  3.9 4.2 %collective-permute-start.1 = (f32[16,1,256]{2,0,1:T(8,128)S(1)}, f32[16,1,256]{2,0,1:T(8,128)S(1)}, u32[]{:S(2)}, u32[]{:S(2)}) collective-permute-start(f32[16,1,256]{2,0,1:T(8,128)S(1)} %get-tuple-element.626), channel_id=1, source_target_pairs={{1,0},{2,1},{3,2},{4,3},{5,4},{6,5},{7,6},{0,7},{9,8},{10,9},{11,1... | collective-permute-start | bytes 49160 | tf_op jit(solution)/shard_map/ppermute | solution.py:97
  8.3 5.4 %collective-permute-start.2 = (f32[16,1,256]{2,1,0:T(1,128)S(1)}, f32[16,1,256]{2,1,0:T(1,128)S(1)}, u32[]{:S(2)}, u32[]{:S(2)}) collective-permute-start(f32[16,1,256]{2,1,0:T(1,128)S(1)} %get-tuple-element.623), channel_id=1, source_target_pairs={{0,1},{1,2},{2,3},{3,4},{4,5},{5,6},{6,7},{7,0},{8,9},{9,10},{10,1... | collective-permute-start | bytes 49160 | tf_op jit(solution)/shard_map/ppermute | solution.py:94
  8.9 4.8 %collective-permute-start.3 = (f32[16,1,256]{2,1,0:T(1,128)S(1)}, f32[16,1,256]{2,1,0:T(1,128)S(1)}, u32[]{:S(2)}, u32[]{:S(2)}) collective-permute-start(f32[16,1,256]{2,1,0:T(1,128)S(1)} %get-tuple-element.624), channel_id=1, source_target_pairs={{1,0},{2,1},{3,2},{4,3},{5,4},{6,5},{7,6},{0,7},{9,8},{10,9},{11,1... | collective-permute-start | bytes 49160 | tf_op jit(solution)/shard_map/ppermute | solution.py:97
  13.8 5.4 %collective-permute-start.4 = (f32[16,1,256]{2,1,0:T(1,128)S(1)}, f32[16,1,256]{2,1,0:T(1,128)S(1)}, u32[]{:S(2)}, u32[]{:S(2)}) collective-permute-start(f32[16,1,256]{2,1,0:T(1,128)S(1)} %get-tuple-element.621), channel_id=1, source_target_pairs={{0,1},{1,2},{2,3},{3,4},{4,5},{5,6},{6,7},{7,0},{8,9},{9,10},{10,1... | collective-permute-start | bytes 49160 | tf_op jit(solution)/shard_map/ppermute | solution.py:94
  13.9 5.3 %collective-permute-start.5 = (f32[16,1,256]{2,1,0:T(1,128)S(1)}, f32[16,1,256]{2,1,0:T(1,128)S(1)}, u32[]{:S(2)}, u32[]{:S(2)}) collective-permute-start(f32[16,1,256]{2,1,0:T(1,128)S(1)} %get-tuple-element.622), channel_id=1, source_target_pairs={{1,0},{2,1},{3,2},{4,3},{5,4},{6,5},{7,6},{0,7},{9,8},{10,9},{11,1... | collective-permute-start | bytes 49160 | tf_op jit(solution)/shard_map/ppermute | solution.py:97
  19.4 5.3 %collective-permute-start.8 = (f32[4,1,256]{2,1,0:T(1,128)S(1)}, f32[4,1,256]{2,1,0:T(1,128)S(1)}, u32[]{:S(2)}, u32[]{:S(2)}) collective-permute-start(f32[4,1,256]{2,1,0:T(1,128)S(1)} %get-tuple-element.629), channel_id=1, source_target_pairs={{0,1},{1,2},{2,3},{3,4},{4,5},{5,6},{6,7},{7,0},{8,9},{9,10},{10,1... | collective-permute-start | bytes 12296 | tf_op jit(solution)/shard_map/ppermute | solution.py:94
  19.4 5.2 %collective-permute-start.9 = (f32[4,1,256]{2,1,0:T(1,128)S(1)}, f32[4,1,256]{2,1,0:T(1,128)S(1)}, u32[]{:S(2)}, u32[]{:S(2)}) collective-permute-start(f32[4,1,256]{2,1,0:T(1,128)S(1)} %get-tuple-element.630), channel_id=1, source_target_pairs={{1,0},{2,1},{3,2},{4,3},{5,4},{6,5},{7,6},{0,7},{9,8},{10,9},{11,1... | collective-permute-start | bytes 12296 | tf_op jit(solution)/shard_map/ppermute | solution.py:97
  30.8 81.8 %all-to-all-start = ((f32[1,1,32,128]{3,1,0,2:T(1,128)}), f32[1,1,32,128]{3,1,0,2:T(1,128)S(1)}, u32[]{:S(2)}, u32[]{:S(2)}) async-start(f32[1,1,32,128]{3,1,0,2:T(1,128)} %bitcast.84), calls=%async_computation | async-start | bytes 32768 | tf_op jit(solution)/shard_map/all_to_all | solution.py:335
  112.6 10.3 %all-to-all-start.2 = ((f32[2,1,32,128]{3,1,0,2:T(1,128)}), f32[2,1,32,128]{3,1,0,2:T(1,128)S(1)}, u32[]{:S(2)}, u32[]{:S(2)}) async-start(f32[2,1,32,128]{3,1,0,2:T(1,128)} %copy.99), calls=%async_computation.2 | async-start | bytes 65536 | tf_op jit(solution)/shard_map/all_to_all | solution.py:334
  115.4 23.9 %copy-start.13 = (f32[19,1]{0,1:T(1,128)S(1)}, f32[19,1]{0,1:T(1,128)}, u32[]{:S(2)}) copy-start(f32[19,1]{0,1:T(1,128)} %constant.279.clone) | copy-start | bytes 232
  115.4 23.9 %copy-start.14 = (f32[19,1]{0,1:T(1,128)S(1)}, f32[19,1]{0,1:T(1,128)}, u32[]{:S(2)}) copy-start(f32[19,1]{0,1:T(1,128)} %constant.280.clone) | copy-start | bytes 232
  122.9 16.5 %all-to-all-start.1 = ((f32[4,4,32,128]{3,1,0,2:T(4,128)}), f32[4,4,32,128]{3,1,0,2:T(4,128)S(1)}, u32[]{:S(2)}, u32[]{:S(2)}) async-start(f32[4,4,32,128]{3,1,0,2:T(4,128)} %copy.98), calls=%async_computation.1 | async-start | bytes 524288 | tf_op jit(solution)/shard_map/all_to_all | solution.py:333
  128.9 17.1 %collective-permute-start.6 = (f32[16,1,256]{2,1,0:T(1,128)S(1)}, f32[16,1,256]{2,1,0:T(1,128)S(1)}, u32[]{:S(2)}, u32[]{:S(2)}) collective-permute-start(f32[16,1,256]{2,1,0:T(1,128)S(1)} %get-tuple-element.619), channel_id=1, source_target_pairs={{0,1},{1,2},{2,3},{3,4},{4,5},{5,6},{6,7},{7,0},{8,9},{9,10},{10,1... | collective-permute-start | bytes 49160 | tf_op jit(solution)/shard_map/ppermute | solution.py:94
  130.3 15.7 %collective-permute-start.7 = (f32[16,1,256]{2,1,0:T(1,128)S(1)}, f32[16,1,256]{2,1,0:T(1,128)S(1)}, u32[]{:S(2)}, u32[]{:S(2)}) collective-permute-start(f32[16,1,256]{2,1,0:T(1,128)S(1)} %get-tuple-element.620), channel_id=1, source_target_pairs={{1,0},{2,1},{3,2},{4,3},{5,4},{6,5},{7,6},{0,7},{9,8},{10,9},{11,1... | collective-permute-start | bytes 49160 | tf_op jit(solution)/shard_map/ppermute | solution.py:97
  143.4 9.8 %all-to-all-start.3 = ((f32[4,32,128]{2,0,1:T(4,128)}), f32[4,32,128]{2,0,1:T(4,128)S(1)}, u32[]{:S(2)}, u32[]{:S(2)}) async-start(f32[4,32,128]{2,0,1:T(4,128)} %concatenate.208), calls=%async_computation.3 | async-start | bytes 131072 | tf_op jit(solution)/shard_map/all_to_all | solution.py:347
  153.4 5.3 %collective-permute-start.10 = (f32[16,1,256]{2,1,0:T(1,128)S(1)}, f32[16,1,256]{2,1,0:T(1,128)S(1)}, u32[]{:S(2)}, u32[]{:S(2)}) collective-permute-start(f32[16,1,256]{2,1,0:T(1,128)S(1)} %get-tuple-element.617), channel_id=1, source_target_pairs={{0,1},{1,2},{2,3},{3,4},{4,5},{5,6},{6,7},{7,0},{8,9},{9,10},{10,1... | collective-permute-start | bytes 49160 | tf_op jit(solution)/shard_map/ppermute | solution.py:94
  154.0 4.8 %collective-permute-start.11 = (f32[16,1,256]{2,1,0:T(1,128)S(1)}, f32[16,1,256]{2,1,0:T(1,128)S(1)}, u32[]{:S(2)}, u32[]{:S(2)}) collective-permute-start(f32[16,1,256]{2,1,0:T(1,128)S(1)} %get-tuple-element.618), channel_id=1, source_target_pairs={{1,0},{2,1},{3,2},{4,3},{5,4},{6,5},{7,6},{0,7},{9,8},{10,9},{11,1... | collective-permute-start | bytes 49160 | tf_op jit(solution)/shard_map/ppermute | solution.py:97
  158.9 5.3 %collective-permute-start.12 = (f32[16,1,256]{2,1,0:T(1,128)S(1)}, f32[16,1,256]{2,1,0:T(1,128)S(1)}, u32[]{:S(2)}, u32[]{:S(2)}) collective-permute-start(f32[16,1,256]{2,1,0:T(1,128)S(1)} %get-tuple-element.615), channel_id=1, source_target_pairs={{0,1},{1,2},{2,3},{3,4},{4,5},{5,6},{6,7},{7,0},{8,9},{9,10},{10,1... | collective-permute-start | bytes 49160 | tf_op jit(solution)/shard_map/ppermute | solution.py:94
  158.9 5.3 %collective-permute-start.13 = (f32[16,1,256]{2,1,0:T(1,128)S(1)}, f32[16,1,256]{2,1,0:T(1,128)S(1)}, u32[]{:S(2)}, u32[]{:S(2)}) collective-permute-start(f32[16,1,256]{2,1,0:T(1,128)S(1)} %get-tuple-element.616), channel_id=1, source_target_pairs={{1,0},{2,1},{3,2},{4,3},{5,4},{6,5},{7,6},{0,7},{9,8},{10,9},{11,1... | collective-permute-start | bytes 49160 | tf_op jit(solution)/shard_map/ppermute | solution.py:97
  164.4 5.3 %collective-permute-start.14 = (f32[4,1,256]{2,1,0:T(1,128)S(1)}, f32[4,1,256]{2,1,0:T(1,128)S(1)}, u32[]{:S(2)}, u32[]{:S(2)}) collective-permute-start(f32[4,1,256]{2,1,0:T(1,128)S(1)} %get-tuple-element.627), channel_id=1, source_target_pairs={{0,1},{1,2},{2,3},{3,4},{4,5},{5,6},{6,7},{7,0},{8,9},{9,10},{10,1... | collective-permute-start | bytes 12296 | tf_op jit(solution)/shard_map/ppermute | solution.py:94
  164.4 5.2 %collective-permute-start.15 = (f32[4,1,256]{2,1,0:T(1,128)S(1)}, f32[4,1,256]{2,1,0:T(1,128)S(1)}, u32[]{:S(2)}, u32[]{:S(2)}) collective-permute-start(f32[4,1,256]{2,1,0:T(1,128)S(1)} %get-tuple-element.628), channel_id=1, source_target_pairs={{1,0},{2,1},{3,2},{4,3},{5,4},{6,5},{7,6},{0,7},{9,8},{10,9},{11,1... | collective-permute-start | bytes 12296 | tf_op jit(solution)/shard_map/ppermute | solution.py:97
  175.8 106.6 %all-to-all-start.4 = ((f32[1,1,32,128]{3,1,0,2:T(1,128)}), f32[1,1,32,128]{3,1,0,2:T(1,128)S(1)}, u32[]{:S(2)}, u32[]{:S(2)}) async-start(f32[1,1,32,128]{3,1,0,2:T(1,128)} %bitcast.93), calls=%async_computation.4 | async-start | bytes 32768 | tf_op jit(solution)/shard_map/all_to_all | solution.py:335
  282.4 10.0 %all-to-all-start.6 = ((f32[2,1,32,128]{3,1,0,2:T(1,128)}), f32[2,1,32,128]{3,1,0,2:T(1,128)S(1)}, u32[]{:S(2)}, u32[]{:S(2)}) async-start(f32[2,1,32,128]{3,1,0,2:T(1,128)} %copy.113), calls=%async_computation.6 | async-start | bytes 65536 | tf_op jit(solution)/shard_map/all_to_all | solution.py:334
  (17 other events, 184.6 us)
where the time goes:
time: 314 us; the launch traced here: 313 us
  starting transfers between devices  225 us (72%)
  local copies, waits for them, and re-layouts  33.1 us (11%)
  waiting for transfers between devices  31.6 us (10%)
  blocking collectives  15.6 us (5%)
  other arithmetic  6.63 us (2%)
    all_to_all x2, starting transfers between devices, forward(): lax.all_to_all(mark_out, ('sec', 'gx'), split_axis=2, concat_axis=2, tile...  175 us
    ppermute x8, starting transfers between devices, padded_2(): lax.ppermute(lax.slice_in_dim(block, 0, width, axis=dim), axis, backward)  30.4 us
    cond x4, local copies, waits for them, and re-layouts, forward(): lax.cond(is_ocean, build, silent, (current, zonal_padded))  16.6 us
    all_to_all x1, blocking collectives, forward(): lax.all_to_all(vol_out, ('sec', 'gx'), split_axis=2, concat_axis=2, tiled...  15.6 us
    another operation x11, local copies, waits for them, and re-layouts  12.6 us
    all_to_all x2, waiting for transfers between devices, forward(): lax.all_to_all(mark_out, ('sec', 'gx'), split_axis=2, concat_axis=2, tile...  10.8 us
    ppermute x8, waiting for transfers between devices, padded_2(): lax.ppermute(lax.slice_in_dim(block, block.shape[dim] - width, None, axis...  7.15 us
    all_to_all x1, waiting for transfers between devices, backward(): lax.all_to_all(outgoing, ('sec', 'gx'), split_axis=1, concat_axis=1, tile...  7.06 us
  transfers between devices with their start and end apart: 22, of which 12 were waited for; matrix products, arithmetic and copies ran while one was open for 6% of the time, Pallas kernels for 0%

commit v1 on v0

v1 whole, which is shorter than its diff:
```python
import functools

import jax
import jax.numpy as jnp
import numpy as np
from jax import lax
from jax.experimental import pallas as pl
from jax.experimental.pallas import tpu as pltpu
from jax.sharding import PartitionSpec as P

STEPS = 2


DT_OCEAN = 0.15
VISCOSITY = 0.2
DIFFUSIVITY = 0.15
DAMPING = 0.05
CORIOLIS = 0.8
HEAT_GAIN = 4.0
ONE_THIRD = 1.0 / 3.0
TWO_THIRDS = 2.0 / 3.0
DT_BIO = 0.8
W_LIMIT = 0.35
W_GAIN = 0.25
KV_BASE = 0.05
KV_SHEAR = 0.3
GAS_RATE = 0.5
WATER_ATTEN = 0.15
CHLORO_ATTEN = 0.1
HEATUP_PER_STEP = 0.5
GROWTH = 0.6
GRAZING = 0.4
REMINERAL = 0.2
EXCRETION = 0.1
PHYTO_LOSS = 0.05
ZOO_LOSS = 0.05
ASSIMILATE = 0.6
YIELDS = np.array(
    [
        0.0,
        0.0,
        0.0,
        0.0,
        -1.3,
        1.0,
        0.16,
        0.9,
        -0.6,
        0.4,
        1.2,
        -0.8,
        0.5,
        0.3,
        -0.4,
        0.7,
        -1.0,
        0.2,
        0.6,
    ],
    np.float32,
)
DECAYS = np.array(
    [
        0.0,
        0.0,
        0.0,
        0.0,
        0.02,
        0.01,
        0.05,
        0.03,
        0.08,
        0.04,
        0.02,
        0.06,
        0.1,
        0.03,
        0.07,
        0.05,
        0.02,
        0.09,
        0.04,
    ],
    np.float32,
)
GAS_ON = np.array([0, 0, 0, 0, 1, 1] + [0] * 13, np.float32)
SOLUBILITY_BASE = np.array([0, 0, 0, 0, 1.2, 1.0] + [0] * 13, np.float32)
SOLUBILITY_HEAT = np.array([0, 0, 0, 0, -0.5, -0.3] + [0] * 13, np.float32)
SOLUBILITY_BRINE = np.array([0, 0, 0, 0, 0.1, 0.3] + [0] * 13, np.float32)

MESH = pl.DeviceIdType.MESH
HALO = 8
LANES = 128
ROWS_SENT = 16


def minmod(one_side, other_side):
    return jnp.maximum(0.0, jnp.minimum(one_side, other_side)) + jnp.minimum(
        0.0, jnp.maximum(one_side, other_side)
    )


def transport_weights(upwelling):
    return [
        None
        if w is None
        else (jnp.maximum(w, 0.0), jnp.minimum(w, 0.0), 0.5 * (1.0 - DT_BIO * jnp.abs(w)))
        for w in upwelling
    ]


def transport(column, weights, mixing):
    levels = len(column)
    diffs = [column[k + 1] - column[k] for k in range(levels - 1)]
    slopes = [None] + [minmod(diffs[k], diffs[k - 1]) for k in range(1, levels - 1)] + [None]
    flux = [None] * (levels + 1)
    for k in range(1, levels):
        up, down, half = weights[k]
        from_below = column[k] if slopes[k] is None else column[k] - half * slopes[k]
        from_above = column[k - 1] if slopes[k - 1] is None else column[k - 1] + half * slopes[k - 1]
        flux[k] = up * from_below + down * from_above + mixing[k] * diffs[k - 1]
    out = []
    for k in range(levels):
        if k == 0:
            gain = flux[1]
        elif k == levels - 1:
            gain = -flux[k]
        else:
            gain = flux[k + 1] - flux[k]
        out.append(column[k] + DT_BIO * gain)
    return out


def light_profile(phyto, sunlight):
    mids, heats = [], []
    top = sunlight
    for p in phyto:
        extinction = WATER_ATTEN + CHLORO_ATTEN * jnp.abs(p)
        mid_pass = jnp.exp(-0.5 * extinction)
        mids.append(top * mid_pass)
        after = top * jnp.exp(-extinction)
        heats.append(top - after)
        top = after
    return mids, heats


def ceil_to(value, unit):
    return (value + unit - 1) // unit * unit


def whole_kernel(
    sections,
    strips,
    levels,
    width,
    lat,
    state_ref,
    heat_ref,
    wind_ref,
    sun_ref,
    sea_ref,
    lists_ref,
    phyto_ref,
    trac_ref,
    out_c,
    out_h,
    grid,
    halo_out,
    halo_in,
    phyto_in,
    placed,
    onehot,
    phyto_grid,
    rim_out,
    rim_in,
    fields,
    send,
    recv,
    halo_ssem,
    halo_rsem,
    phyto_ssem,
    phyto_rsem,
    rim_ssem,
    rim_rsem,
    field_ssem,
    field_rsem,
):
    owners = (sections - 1) * strips
    species = trac_ref.shape[0]
    padded_rows = grid.shape[1]
    sec = lax.axis_index("sec")
    strip = lax.axis_index("gx")
    right = lax.rem(strip + 1, strips)
    left = lax.rem(strip + strips - 1, strips)
    me = (sec - 1) * strips + strip
    lat_shift = lat.bit_length() - 1
    halves = lat // LANES
    place_rows = placed.shape[0] // (3 * levels)
    first_heat = 4 * levels
    first_wind = 5 * levels
    sun_row = first_wind + 2
    sea_row = first_wind + 3

    @pl.when(sec == 0)
    def _():
        out_c[...] = trac_ref[...]
        out_h[...] = jnp.zeros_like(out_h)

    @pl.when(sec > 0)
    def _():
        def channel(c, rows):
            if c < first_heat:
                return state_ref[c, rows, :]
            if c < first_wind:
                return heat_ref[c - first_heat, rows, :]
            if c < sun_row:
                return wind_ref[c - first_wind, rows, :]
            if c == sun_row:
                return sun_ref[rows, :]
            return sea_ref[rows, :].astype(jnp.float32)

        for c in range(grid.shape[0]):
            halo_out[0, c] = channel(c, slice(width - HALO, width))
            halo_out[1, c] = channel(c, slice(0, HALO))

        barrier = pltpu.get_barrier_semaphore()

        def greet(i, carry):
            t = lax.rem(me + i, owners)
            pl.semaphore_signal(
                barrier, inc=1, device_id=(1 + t // strips, lax.rem(t, strips)), device_id_type=MESH
            )
            return carry

        lax.fori_loop(1, owners, greet, 0)
        pl.semaphore_wait(barrier, owners - 1)

        def edge_copy(out_ref, in_ref, ssem, rsem, side):
            return pltpu.make_async_remote_copy(
                src_ref=out_ref.at[side],
                dst_ref=in_ref.at[side],
                send_sem=ssem.at[side],
                recv_sem=rsem.at[side],
                device_id=(sec, right if side == 0 else left),
                device_id_type=MESH,
            )

        halo_copies = [
            edge_copy(halo_out, halo_in, halo_ssem, halo_rsem, side) for side in range(2)
        ]

        def phyto_copy(t, slot):
            target = lax.rem(t, strips)
            return pltpu.make_async_remote_copy(
                src_ref=phyto_ref.at[:, pl.ds(pl.multiple_of(target * LANES, LANES), LANES)],
                dst_ref=phyto_in.at[slot],
                send_sem=phyto_ssem.at[t],
                recv_sem=phyto_rsem.at[slot],
                device_id=(1 + t // strips, target),
                device_id_type=MESH,
            )

        def send_phyto(i, carry):
            phyto_copy(lax.rem(me + i, owners), me).start()
            return carry

        lax.fori_loop(1, owners, send_phyto, 0)
        for copy in halo_copies:
            copy.start()

        phyto_in[me] = phyto_ref[:, pl.ds(pl.multiple_of(strip * LANES, LANES), LANES)]

        for c in range(grid.shape[0]):
            if padded_rows > width + 2 * HALO:
                grid[c, width + 2 * HALO :, :] = jnp.zeros(
                    (padded_rows - width - 2 * HALO, lat), jnp.float32
                )
            grid[c, HALO : HALO + width, :] = channel(c, slice(0, width))

        def wait_phyto(i, carry):
            t = lax.rem(me + i, owners)
            phyto_copy(t, t).wait()
            return carry

        lax.fori_loop(1, owners, wait_phyto, 0)

        lat_index = lax.broadcasted_iota(jnp.int32, (lat, LANES), 0)
        lon_index = lax.broadcasted_iota(jnp.int32, (place_rows, LANES), 0)

        def spread(l, carry):
            listed = lists_ref[pl.ds(l, 1), :]
            x = listed >> lat_shift
            y = listed & (lat - 1)
            lanes = pl.ds(pl.multiple_of(l * LANES, LANES), LANES)
            onehot[:, lanes] = jnp.where(lat_index == y, 1.0, 0.0).astype(jnp.bfloat16)
            here = lon_index == x
            values = phyto_in[l]
            for k in range(levels):
                rest = values[k : k + 1, :]
                for part in range(3):
                    term = rest.astype(jnp.bfloat16).astype(jnp.float32)
                    rest = rest - term
                    row = (3 * k + part) * place_rows
                    placed[row : row + place_rows, lanes] = jnp.where(here, term, 0.0).astype(
                        jnp.bfloat16
                    )
            return carry

        lax.fori_loop(0, owners, spread, 0)
        spread_out = lax.dot_general(
            placed[...],
            onehot[...],
            (((1,), (1,)), ((), ())),
            preferred_element_type=jnp.float32,
        )
        for k in range(levels):
            base = 3 * k * place_rows
            own = (
                spread_out[base : base + width]
                + spread_out[base + place_rows : base + place_rows + width]
                + spread_out[base + 2 * place_rows : base + 2 * place_rows + width]
            )
            phyto_grid[k] = jnp.zeros((padded_rows, lat), jnp.float32)
            phyto_grid[k, HALO : HALO + width, :] = own
            rim_out[0, 2 * k : 2 * k + 2, :] = own[width - 2 : width]
            rim_out[1, 2 * k : 2 * k + 2, :] = own[0:2]

        rim_copies = [edge_copy(rim_out, rim_in, rim_ssem, rim_rsem, side) for side in range(2)]
        for copy in rim_copies:
            copy.start()
        for copy in halo_copies:
            copy.wait()
        for c in range(grid.shape[0]):
            grid[c, 0:HALO, :] = halo_in[0, c]
            grid[c, HALO + width : 2 * HALO + width, :] = halo_in[1, c]

        lane = lax.broadcasted_iota(jnp.int32, (padded_rows, lat), 1)
        not_last = lane < lat - 1
        not_first = lane > 0
        coriolis_y = CORIOLIS * (2.0 * (lane.astype(jnp.float32) + 0.5) / lat - 1.0)

        def around(field):
            east = pltpu.roll(field, padded_rows - 1, 0)
            west = pltpu.roll(field, 1, 0)
            north = jnp.where(not_last, pltpu.roll(field, lat - 1, 1), 0.0)
            south = jnp.where(not_first, pltpu.roll(field, 1, 1), 0.0)
            return east, west, north, south

        def rates(u, v, q, r, heating, k):
            def flow(field):
                east, west, north, south = around(field)
                return east + west + north + south - 4.0 * field

            def carried(field):
                east, west, north, south = around(field)
                return (
                    DIFFUSIVITY * (east + west + north + south - 4.0 * field)
                    - (u * (0.5 * (east - west)) + v * (0.5 * (north - south)))
                )

            sea = grid[sea_row]
            du = coriolis_y * v - DAMPING * u + VISCOSITY * flow(u)
            dv = -coriolis_y * u - DAMPING * v + VISCOSITY * flow(v)
            if k == 0:
                du = du + grid[first_wind]
                dv = dv + grid[first_wind + 1]
            dq = carried(q) + HEAT_GAIN * heating
            dr = carried(r)
            return [sea * d for d in (du, dv, dq, dr)]

        def ocean_step():
            for k in range(levels):
                start = [grid[f * levels + k] for f in range(4)]
                heating = grid[first_heat + k]
                first = [s + DT_OCEAN * d for s, d in zip(start, rates(*start, heating, k))]
                second = [
                    0.75 * s + 0.25 * (f + DT_OCEAN * d)
                    for s, f, d in zip(start, first, rates(*first, heating, k))
                ]
                third = [
                    ONE_THIRD * s + TWO_THIRDS * (f + DT_OCEAN * d)
                    for s, f, d in zip(start, second, rates(*second, heating, k))
                ]
                for f in range(4):
                    grid[f * levels + k] = third[f]

        def column_fields():
            total = None
            for k in range(levels - 1, 0, -1):
                u, v = grid[k], grid[levels + k]
                east = pltpu.roll(u, padded_rows - 1, 0)
                west = pltpu.roll(u, 1, 0)
                north = jnp.where(not_last, pltpu.roll(v, lat - 1, 1), 0.0)
                south = jnp.where(not_first, pltpu.roll(v, 1, 1), 0.0)
                div = 0.5 * (east - west) + 0.5 * (north - south)
                total = div if total is None else total + div
                fields[k - 1] = W_LIMIT * jnp.tanh(W_GAIN * total)
                shear = (u - grid[k - 1]) ** 2 + (v - grid[levels + k - 1]) ** 2
                fields[levels - 1 + k - 1] = KV_BASE + KV_SHEAR * shear / (1.0 + shear)

        fields[2 * (levels - 1)] = (
            grid[first_wind] * grid[first_wind] + grid[first_wind + 1] * grid[first_wind + 1]
        )

        def sent_channels():
            refs = [(grid, 2 * levels + i) for i in range(2 * levels)]
            refs += [(fields, i) for i in range(2 * levels - 1)]
            refs += [(grid, sun_row)]
            return refs

        tile_count = ceil_to(width, 8) // 8
        sublane = lax.broadcasted_iota(jnp.int32, (8, LANES), 0)

        def field_copy(step, h, slot):
            return pltpu.make_async_remote_copy(
                src_ref=send.at[step, h],
                dst_ref=recv.at[step, slot],
                send_sem=field_ssem.at[step, h],
                recv_sem=field_rsem.at[step, slot],
                device_id=(sec, h),
                device_id_type=MESH,
            )

        def pick(step, h):
            listed = lists_ref[pl.ds((sec - 1) * strips + h, 1), :]
            x = jnp.broadcast_to(listed >> lat_shift, (8, LANES))
            y = jnp.broadcast_to(listed & (lat - 1), (8, LANES))
            low = y & (LANES - 1)
            half = y >> (LANES.bit_length() - 1)
            for c, (ref, row) in enumerate(sent_channels()):
                total = jnp.zeros((8, LANES), jnp.float32)
                for tile in range(tile_count):
                    rows = slice(HALO + 8 * tile, HALO + 8 * tile + 8)
                    for part in range(halves):
                        taken = jnp.take_along_axis(
                            ref[row, rows, part * LANES : (part + 1) * LANES],
                            low,
                            axis=1,
                            mode="promise_in_bounds",
                        )
                        mine = (x == sublane + 8 * tile) & (half == part)
                        total = jnp.where(mine, taken, total)
                send[step, h, c : c + 1, :] = jnp.sum(total, axis=0, keepdims=True)

        def send_fields(step):
            def one(i, carry):
                h = lax.rem(strip + i, strips)
                pick(step, h)
                field_copy(step, h, strip).start()
                return carry

            lax.fori_loop(1, strips, one, 0)
            pick(step, strip)
            recv[step, strip] = send[step, strip]

        def wait_fields(step):
            def one(i, carry):
                h = lax.rem(strip + i, strips)
                field_copy(step, h, h).wait()
                return carry

            lax.fori_loop(1, strips, one, 0)

        def advance(step, source, last):
            def received(c):
                return jnp.concatenate(
                    [recv[step, h, c : c + 1, :] for h in range(strips)], axis=0
                )

            heat_now = [received(k) for k in range(levels)]
            salt_top = received(levels)
            base = 2 * levels
            weights = transport_weights(
                [None] + [received(base + k) for k in range(levels - 1)]
            )
            mixing = [None] + [received(base + levels - 1 + k) for k in range(levels - 1)]
            power = received(base + 2 * (levels - 1))
            sunlight = received(ROWS_SENT - 1)
            valid = sunlight > 0.5
            transfer = GAS_RATE * power / (1.0 + power)

            before = [[source[n, k] for k in range(levels)] for n in range(4)]
            moved = [transport(column, weights, mixing) for column in before]
            mids, heats = light_profile(moved[1], sunlight)
            surplus = []
            for k in range(levels):
                n_, p_, z_, d_ = (moved[i][k] for i in range(4))
                warm = jnp.exp(HEATUP_PER_STEP * heat_now[k])
                growth = (
                    GROWTH * warm * mids[k] / (mids[k] + 1.0) * jnp.abs(n_) / (jnp.abs(n_) + 1.0) * p_
                )
                grazing = GRAZING * warm * p_ * p_ / (p_ * p_ + 1.0) * z_
                remineral = REMINERAL * warm * d_
                changes = (
                    -growth + remineral + EXCRETION * z_,
                    growth - grazing - PHYTO_LOSS * p_,
                    ASSIMILATE * grazing - EXCRETION * z_ - ZOO_LOSS * z_,
                    (1.0 - ASSIMILATE) * grazing + PHYTO_LOSS * p_ + ZOO_LOSS * z_ - remineral,
                )
                for i in range(4):
                    out_c[i, k] = jnp.where(
                        valid, moved[i][k] + DT_BIO * changes[i], before[i][k]
                    )
                surplus.append(remineral - growth)
                if last:
                    out_h[k] = jnp.where(valid, heats[k], 0.0)
            for n in range(4, species):
                column = [source[n, k] for k in range(levels)]
                now = transport(column, weights, mixing)
                if GAS_ON[n]:
                    limit = (
                        float(SOLUBILITY_BASE[n])
                        + float(SOLUBILITY_HEAT[n]) * heat_now[0]
                        + float(SOLUBILITY_BRINE[n]) * salt_top
                    )
                    now[0] = now[0] + DT_BIO * transfer * (limit - now[0])
                for k in range(levels):
                    change = float(YIELDS[n]) * surplus[k] - float(DECAYS[n]) * now[k]
                    out_c[n, k] = jnp.where(valid, now[k] + DT_BIO * change, column[k])

        for step in range(STEPS):
            ocean_step()
            column_fields()
            send_fields(step)
            if step == 0:
                for copy in rim_copies:
                    copy.wait()
                for k in range(levels):
                    phyto_grid[k, HALO - 2 : HALO, :] = rim_in[0, 2 * k : 2 * k + 2, :]
                    phyto_grid[k, HALO + width : HALO + width + 2, :] = rim_in[
                        1, 2 * k : 2 * k + 2, :
                    ]
                weights = transport_weights([None] + [fields[k] for k in range(levels - 1)])
                mixing = [None] + [fields[levels - 1 + k] for k in range(levels - 1)]
                moved = transport([phyto_grid[k] for k in range(levels)], weights, mixing)
                _, heats = light_profile(moved, grid[sun_row])
                for k in range(levels):
                    grid[first_heat + k] = heats[k]
        wait_fields(0)
        advance(0, trac_ref, False)
        wait_fields(1)
        advance(1, out_c, True)


def per_device(ocean_state, heat_first, wind_stress, shortwave, sea_mask, owner_cols, tracers):
    sections = lax.axis_size("sec")
    strips = lax.axis_size("gx")
    fields_count, levels, width, lat = ocean_state.shape
    owners = (sections - 1) * strips
    species = tracers.shape[0]
    padded_rows = ceil_to(width + 2 * HALO, 8)
    place_rows = ceil_to(width, 16)
    channels = 5 * levels + 4
    f32 = jnp.float32
    vmem = pl.BlockSpec(memory_space=pltpu.VMEM)
    new_c, new_h = pl.pallas_call(
        functools.partial(whole_kernel, sections, strips, levels, width, lat),
        out_shape=(
            jax.ShapeDtypeStruct((species, levels, strips, LANES), f32),
            jax.ShapeDtypeStruct((levels, strips, LANES), f32),
        ),
        in_specs=[vmem] * 8,
        out_specs=(vmem, vmem),
        scratch_shapes=[
            pltpu.VMEM((channels, padded_rows, lat), f32),
            pltpu.VMEM((2, channels, HALO, lat), f32),
            pltpu.VMEM((2, channels, HALO, lat), f32),
            pltpu.VMEM((owners, levels, LANES), f32),
            pltpu.VMEM((3 * levels * place_rows, owners * LANES), jnp.bfloat16),
            pltpu.VMEM((lat, owners * LANES), jnp.bfloat16),
            pltpu.VMEM((levels, padded_rows, lat), f32),
            pltpu.VMEM((2, 2 * levels, lat), f32),
            pltpu.VMEM((2, 2 * levels, lat), f32),
            pltpu.VMEM((2 * levels - 1, padded_rows, lat), f32),
            pltpu.VMEM((STEPS, strips, ROWS_SENT, LANES), f32),
            pltpu.VMEM((STEPS, strips, ROWS_SENT, LANES), f32),
            pltpu.SemaphoreType.DMA((2,)),
            pltpu.SemaphoreType.DMA((2,)),
            pltpu.SemaphoreType.DMA((owners,)),
            pltpu.SemaphoreType.DMA((owners,)),
            pltpu.SemaphoreType.DMA((2,)),
            pltpu.SemaphoreType.DMA((2,)),
            pltpu.SemaphoreType.DMA((STEPS, strips)),
            pltpu.SemaphoreType.DMA((STEPS, strips)),
        ],
        compiler_params=pltpu.CompilerParams(
            collective_id=0, has_side_effects=True, vmem_limit_bytes=56 << 20
        ),
    )(
        ocean_state.reshape(fields_count * levels, width, lat),
        heat_first,
        wind_stress,
        shortwave,
        sea_mask,
        owner_cols.reshape(owners, LANES),
        tracers[1],
        tracers.reshape(species, levels, strips, LANES),
    )
    return new_c.reshape(tracers.shape), new_h.reshape(levels, -1)


def solution(mesh):
    return jax.shard_map(
        per_device,
        mesh=mesh,
        in_specs=(
            P(None, None, "gx", None),
            P(None, "gx", None),
            P(None, "gx", None),
            P("gx", None),
            P("gx", None),
            P("gx", None, None, None),
            P(None, None, ("sec", "gx")),
        ),
        out_specs=(P(None, None, ("sec", "gx")), P(None, ("sec", "gx"))),
        check_vma=False,
    )
```

time: 314 us -> 36 us (0.11)
  starting transfers between devices: 225 us -> 0 us
  waiting for transfers between devices: 31.6 us -> 0 us
  Pallas kernels: 0 us -> 27 us
  local copies, waits for them, and re-layouts: 33.1 us -> 8.18 us
  blocking collectives: 15.6 us -> 0 us
  other arithmetic: 6.63 us -> 0 us
    all_to_all x6 -> x0, starting transfers between devices: 189 us -> none  [the longest x2 175 us: forward(): lax.all_to_all(mark_out, ('sec', 'gx'), split_axis=2, concat_axis=2, tile...]
    ppermute x16 -> x0, starting transfers between devices: 35.3 us -> none  [the longest x8 30.4 us: padded_2(): lax.ppermute(lax.slice_in_dim(block, 0, width, axis=dim), axis, backward)]
    pallas_call x0 -> x1, Pallas kernels: none -> 27 us  [per_device(): pl.pallas_call(functools.partial(whole_kernel, sections, strips, levels,...]
    all_to_all x6 -> x0, waiting for transfers between devices: 24.4 us -> none  [the longest x2 10.8 us: forward(): lax.all_to_all(mark_out, ('sec', 'gx'), split_axis=2, concat_axis=2, tile...]
    cond x12 -> x0, local copies, waits for them, and re-layouts: 17.4 us -> none  [the longest x4 16.6 us: forward(): lax.cond(is_ocean, build, silent, (current, zonal_padded))]
    all_to_all x1 -> x0, blocking collectives: 15.6 us -> none  [forward(): lax.all_to_all(vol_out, ('sec', 'gx'), split_axis=2, concat_axis=2, tiled...]
    another operation x11 -> x0, local copies, waits for them, and re-layouts: 12.6 us -> none
    ppermute x16 -> x0, waiting for transfers between devices: 7.17 us -> none  [the longest x8 7.15 us: padded_2(): lax.ppermute(lax.slice_in_dim(block, block.shape[dim] - width, None, axis...]
  transfers between devices with their start and end apart: 22 -> 0, of which waited for: 12 -> 0; matrix products, arithmetic and copies ran while one was open for 6% -> 0% of each run, Pallas kernels for 0% -> 0%
where the time goes in v1:
time: 36 us; the launch traced here: 35.8 us
  Pallas kernels  27 us (75%)
  local copies, waits for them, and re-layouts  8.18 us (23%)
  between operations  0.66 us (2%)
    pallas_call x1, Pallas kernels, per_device(): pl.pallas_call(functools.partial(whole_kernel, sections, strips, levels,...  27 us
    unnamed x10, local copies, waits for them, and re-layouts  4.18 us
    reshape x1, local copies, waits for them, and re-layouts, per_device(): return (new_c.reshape(tracers.shape), new_h.reshape(levels, -1))  1.79 us
    squeeze x1, local copies, waits for them, and re-layouts, per_device(): tracers[1]  1.36 us
    reshape x1, local copies, waits for them, and re-layouts, per_device(): tracers.reshape(species, levels, strips, LANES)  0.84 us

profile of v1, /device:TPU:1, one launch (start us, length us, event | category | flops | bytes accessed | tf_op | source)
XLA Modules:
  0.0 35.8 jit_solution(572866917889817480)
XLA Ops:
  0.6 0.0 copy-start.1
  0.6 1.4 %slice_bitcast_fusion.phyto_ref = f32[4,1024]{1,0:T(4,128)} fusion(f32[19,4,1024]{2,1,0:T(4,128)} %param.13), kind=kLoop, calls=%fused_computation.1 | loop fusion | bytes 32768 | tf_op jit(solution)/shard_map/squeeze | solution.py:596
  2.0 0.0 copy-start
  2.0 1.4 %copy.11.wind_ref = f32[2,12,256]{2,1,0:T(8,128)} copy(f32[2,12,256]{2,0,1:T(2,128)} %param.9) | data formatting | bytes 49152 | tf_op args[2]
  3.4 1.4 %copy.10.heat_ref = f32[4,12,256]{2,1,0:T(8,128)} copy(f32[4,12,256]{2,0,1:T(4,128)} %param.8) | data formatting | bytes 98304 | tf_op args[1]
  4.8 0.0 copy-done.1
  4.8 0.7 %copy.9 = f32[4,4,12,256]{3,2,1,0:T(8,128)} copy(f32[4,4,12,256]{3,1,2,0:T(4,128)S(1)} %copy-done.1) | data formatting | bytes 393216 | tf_op args[0]
  5.6 0.0 copy-done
  5.6 0.8 %reshape.21.trac_ref = f32[19,4,8,128]{3,2,1,0:T(8,128)} reshape(f32[19,4,1024]{2,1,0:T(4,128)S(1)} %copy-done) | data formatting | bytes 622592 | tf_op jit(solution)/shard_map/reshape | solution.py:597
  6.4 27.0 %shard_map.86 = (f32[19,4,8,128]{3,2,1,0:T(8,128)}, f32[4,8,128]{2,1,0:T(8,128)}) custom-call(f32[16,12,256]{2,1,0:T(8,128)} %bitcast.10, f32[4,12,256]{2,1,0:T(8,128)} %copy.10.heat_ref, f32[2,12,256]{2,1,0:T(8,128)} %copy.11.wind_ref, f32[12,256]{1,0:T(8,128)} %sun_ref.1, s32[12,256]{1,0:T(8,128)} %sea_ref.1, s32[24,128]{1,0:T(8,128)} %bitcast.13, ...), custom_call_target="tpu_custom_call" | custom-call | tf_op jit(solution)/shard_map/pallas_call | solution.py:556
  33.4 0.0 copy-start.2
  33.4 1.8 %reshape.22 = f32[19,4,1024]{2,1,0:T(4,128)} reshape(f32[19,4,8,128]{3,2,1,0:T(8,128)} %get-tuple-element.4) | data formatting | bytes 622592 | tf_op jit(solution)/shard_map/reshape | solution.py:599
  35.2 0.0 copy-done.2
  35.2 0.6 %copy.14 = f32[1,4,8,128]{3,1,2,0:T(4,128)} copy(f32[1,4,8,128]{3,2,1,0:T(8,128)S(1)} %bitcast.12) | data formatting | bytes 32768
Async XLA Ops:
  0.6 4.2 %copy-start.1 = (f32[4,4,12,256]{3,1,2,0:T(4,128)S(1)}, f32[4,4,12,256]{3,1,2,0:T(4,128)}, u32[]{:S(2)}) copy-start(f32[4,4,12,256]{3,1,2,0:T(4,128)} %param.7) | copy-start | bytes 589828
  2.0 3.6 %copy-start = (f32[19,4,1024]{2,1,0:T(4,128)S(1)}, f32[19,4,1024]{2,1,0:T(4,128)}, u32[]{:S(2)}) copy-start(f32[19,4,1024]{2,1,0:T(4,128)} %param.13) | copy-start | bytes 933892
  33.4 1.8 %copy-start.2 = (f32[4,8,128]{2,1,0:T(8,128)S(1)}, f32[4,8,128]{2,1,0:T(8,128)}, u32[]{:S(2)}) copy-start(f32[4,8,128]{2,1,0:T(8,128)} %get-tuple-element.5) | copy-start | bytes 49156

commit v2 on v1

--- a/solution.py
+++ b/solution.py
@@ -160,13 +160,13 @@
     sun_ref,
     sea_ref,
     lists_ref,
-    phyto_ref,
     trac_ref,
     out_c,
     out_h,
     grid,
     halo_out,
     halo_in,
+    phyto_out,
     phyto_in,
     placed,
     onehot,
@@ -209,12 +209,30 @@
     @pl.when(sec > 0)
     def _():
         def channel(c, rows):
+            count = rows.stop - rows.start
+
+            def interleaved(ref, lead, group, member):
+                return jnp.concatenate(
+                    [
+                        ref[
+                            pl.ds(
+                                ((lead * width + rows.start) * halves + part) * group + member,
+                                count,
+                                stride=halves * group,
+                            ),
+                            :,
+                        ]
+                        for part in range(halves)
+                    ],
+                    axis=1,
+                )
+
             if c < first_heat:
-                return state_ref[c, rows, :]
+                return interleaved(state_ref, c // levels, levels, c % levels)
             if c < first_wind:
-                return heat_ref[c - first_heat, rows, :]
+                return interleaved(heat_ref, 0, levels, c - first_heat)
             if c < sun_row:
-                return wind_ref[c - first_wind, rows, :]
+                return interleaved(wind_ref, 0, 2, c - first_wind)
             if c == sun_row:
                 return sun_ref[rows, :]
             return sea_ref[rows, :].astype(jnp.float32)
@@ -222,6 +240,9 @@
         for c in range(grid.shape[0]):
             halo_out[0, c] = channel(c, slice(width - HALO, width))
             halo_out[1, c] = channel(c, slice(0, HALO))
+
+        for h in range(strips):
+            phyto_out[h] = trac_ref[1, h * levels : (h + 1) * levels, :]
 
         barrier = pltpu.get_barrier_semaphore()
 
@@ -252,7 +273,7 @@
         def phyto_copy(t, slot):
             target = lax.rem(t, strips)
             return pltpu.make_async_remote_copy(
-                src_ref=phyto_ref.at[:, pl.ds(pl.multiple_of(target * LANES, LANES), LANES)],
+                src_ref=phyto_out.at[target],
                 dst_ref=phyto_in.at[slot],
                 send_sem=phyto_ssem.at[t],
                 recv_sem=phyto_rsem.at[slot],
@@ -268,7 +289,7 @@
         for copy in halo_copies:
             copy.start()
 
-        phyto_in[me] = phyto_ref[:, pl.ds(pl.multiple_of(strip * LANES, LANES), LANES)]
+        phyto_in[me] = phyto_out[strip]
 
         for c in range(grid.shape[0]):
             if padded_rows > width + 2 * HALO:
@@ -414,7 +435,9 @@
         def field_copy(step, h, slot):
             return pltpu.make_async_remote_copy(
                 src_ref=send.at[step, h],
-                dst_ref=recv.at[step, slot],
+                dst_ref=recv.at[
+                    step, pl.ds(pl.multiple_of(slot * ROWS_SENT, ROWS_SENT), ROWS_SENT)
+                ],
                 send_sem=field_ssem.at[step, h],
                 recv_sem=field_rsem.at[step, slot],
                 device_id=(sec, h),
@@ -451,7 +474,9 @@
 
             lax.fori_loop(1, strips, one, 0)
             pick(step, strip)
-            recv[step, strip] = send[step, strip]
+            recv[step, pl.ds(pl.multiple_of(strip * ROWS_SENT, ROWS_SENT), ROWS_SENT), :] = send[
+                step, strip
+            ]
 
         def wait_fields(step):
             def one(i, carry):
@@ -463,9 +488,10 @@
 
         def advance(step, source, last):
             def received(c):
-                return jnp.concatenate(
-                    [recv[step, h, c : c + 1, :] for h in range(strips)], axis=0
-                )
+                return recv[step, pl.ds(c, strips, stride=ROWS_SENT), :]
+
+            def level_rows(k):
+                return pl.ds(k, strips, stride=levels)
 
             heat_now = [received(k) for k in range(levels)]
             salt_top = received(levels)
@@ -479,7 +505,7 @@
             valid = sunlight > 0.5
             transfer = GAS_RATE * power / (1.0 + power)
 
-            before = [[source[n, k] for k in range(levels)] for n in range(4)]
+            before = [[source[n, level_rows(k), :] for k in range(levels)] for n in range(4)]
             moved = [transport(column, weights, mixing) for column in before]
             mids, heats = light_profile(moved[1], sunlight)
             surplus = []
@@ -498,14 +524,14 @@
                     (1.0 - ASSIMILATE) * grazing + PHYTO_LOSS * p_ + ZOO_LOSS * z_ - remineral,
                 )
                 for i in range(4):
-                    out_c[i, k] = jnp.where(
+                    out_c[i, level_rows(k), :] = jnp.where(
                         valid, moved[i][k] + DT_BIO * changes[i], before[i][k]
                     )
                 surplus.append(remineral - growth)
                 if last:
-                    out_h[k] = jnp.where(valid, heats[k], 0.0)
+                    out_h[level_rows(k), :] = jnp.where(valid, heats[k], 0.0)
             for n in range(4, species):
-                column = [source[n, k] for k in range(levels)]
+                column = [source[n, level_rows(k), :] for k in range(levels)]
                 now = transport(column, weights, mixing)
                 if GAS_ON[n]:
                     limit = (
@@ -516,7 +542,7 @@
                     now[0] = now[0] + DT_BIO * transfer * (limit - now[0])
                 for k in range(levels):
                     change = float(YIELDS[n]) * surplus[k] - float(DECAYS[n]) * now[k]
-                    out_c[n, k] = jnp.where(valid, now[k] + DT_BIO * change, column[k])
+                    out_c[n, level_rows(k), :] = jnp.where(valid, now[k] + DT_BIO * change, column[k])
 
         for step in range(STEPS):
             ocean_step()
@@ -551,20 +577,22 @@
     padded_rows = ceil_to(width + 2 * HALO, 8)
     place_rows = ceil_to(width, 16)
     channels = 5 * levels + 4
+    halves = lat // LANES
     f32 = jnp.float32
     vmem = pl.BlockSpec(memory_space=pltpu.VMEM)
     new_c, new_h = pl.pallas_call(
         functools.partial(whole_kernel, sections, strips, levels, width, lat),
         out_shape=(
-            jax.ShapeDtypeStruct((species, levels, strips, LANES), f32),
-            jax.ShapeDtypeStruct((levels, strips, LANES), f32),
+            jax.ShapeDtypeStruct((species, strips * levels, LANES), f32),
+            jax.ShapeDtypeStruct((strips * levels, LANES), f32),
         ),
-        in_specs=[vmem] * 8,
+        in_specs=[vmem] * 7,
         out_specs=(vmem, vmem),
         scratch_shapes=[
             pltpu.VMEM((channels, padded_rows, lat), f32),
             pltpu.VMEM((2, channels, HALO, lat), f32),
             pltpu.VMEM((2, channels, HALO, lat), f32),
+            pltpu.VMEM((strips, levels, LANES), f32),
             pltpu.VMEM((owners, levels, LANES), f32),
             pltpu.VMEM((3 * levels * place_rows, owners * LANES), jnp.bfloat16),
             pltpu.VMEM((lat, owners * LANES), jnp.bfloat16),
@@ -573,7 +601,7 @@
             pltpu.VMEM((2, 2 * levels, lat), f32),
             pltpu.VMEM((2 * levels - 1, padded_rows, lat), f32),
             pltpu.VMEM((STEPS, strips, ROWS_SENT, LANES), f32),
-            pltpu.VMEM((STEPS, strips, ROWS_SENT, LANES), f32),
+            pltpu.VMEM((STEPS, strips * ROWS_SENT, LANES), f32),
             pltpu.SemaphoreType.DMA((2,)),
             pltpu.SemaphoreType.DMA((2,)),
             pltpu.SemaphoreType.DMA((owners,)),
@@ -587,15 +615,20 @@
             collective_id=0, has_side_effects=True, vmem_limit_bytes=56 << 20
         ),
     )(
-        ocean_state.reshape(fields_count * levels, width, lat),
-        heat_first,
-        wind_stress,
+        ocean_state.reshape(fields_count, levels, width, halves, LANES)
+        .transpose(0, 2, 3, 1, 4)
+        .reshape(-1, LANES),
+        heat_first.reshape(levels, width, halves, LANES).transpose(1, 2, 0, 3).reshape(-1, LANES),
+        wind_stress.reshape(2, width, halves, LANES).transpose(1, 2, 0, 3).reshape(-1, LANES),
         shortwave,
         sea_mask,
         owner_cols.reshape(owners, LANES),
-        tracers[1],
-        tracers.reshape(species, levels, strips, LANES),
+        tracers.reshape(species, levels, strips, LANES)
+        .transpose(0, 2, 1, 3)
+        .reshape(species, strips * levels, LANES),
     )
+    new_c = new_c.reshape(species, strips, levels, LANES).transpose(0, 2, 1, 3)
+    new_h = new_h.reshape(strips, levels, LANES).transpose(1, 0, 2)
     return new_c.reshape(tracers.shape), new_h.reshape(levels, -1)
 
 

time: 36 us -> 30.1 us (0.84)
  local copies, waits for them, and re-layouts: 8.18 us -> 2.32 us
    reshape x2 -> x0, local copies, waits for them, and re-layouts: 2.64 us -> none  [the longest x1 1.79 us: per_device(): return (new_c.reshape(tracers.shape), new_h.reshape(levels, -1))]
    unnamed x10 -> x4, local copies, waits for them, and re-layouts: 4.18 us -> 2.32 us
    squeeze x1 -> x0, local copies, waits for them, and re-layouts: 1.36 us -> none  [per_device(): tracers[1]]
where the time goes in v2:
time: 30.1 us; the launch traced here: 29.9 us
  Pallas kernels  27 us (90%)
  local copies, waits for them, and re-layouts  2.32 us (8%)
  between operations  0.65 us (2%)
    pallas_call x1, Pallas kernels, per_device(): pl.pallas_call(functools.partial(whole_kernel, sections, strips, levels,...  27 us
    unnamed x4, local copies, waits for them, and re-layouts  2.32 us

profile of v2, /device:TPU:1, one launch (start us, length us, event | category | flops | bytes accessed | tf_op | source)
XLA Modules:
  0.0 29.9 jit_solution(2541875043512068932)
XLA Ops:
  0.6 27.0 %shard_map.86 = (f32[19,32,128]{2,1,0:T(8,128)}, f32[32,128]{1,0:T(8,128)}) custom-call(f32[384,128]{1,0:T(8,128)} %bitcast.33, f32[96,128]{1,0:T(8,128)} %bitcast.34, f32[48,128]{1,0:T(8,128)} %bitcast.35, f32[12,256]{1,0:T(8,128)} %sun_ref.1, s32[12,256]{1,0:T(8,128)} %sea_ref.1, s32[24,128]{1,0:T(8,128)} %bitcast.37, f32[19,32,128]{2,1,0:T(8,128)} %bitcast.31), custom_call_target="tpu_custom_call" | custom-call | tf_op jit(solution)/shard_map/pallas_call | solution.py:583
  27.6 0.0 copy-start
  27.6 1.7 %copy.17 = f32[19,4,1024]{2,1,0:T(4,128)} copy(f32[19,4,1024]{2,1,0:T(4,128)} %bitcast.32) | data formatting | bytes 622592
  29.3 0.0 copy-done
  29.3 0.6 %copy.18 = f32[4,1024]{1,0:T(4,128)} copy(f32[4,1024]{1,0:T(4,128)S(1)} %bitcast.36) | data formatting | bytes 32768
Async XLA Ops:
  27.6 1.7 %copy-start = (f32[32,128]{1,0:T(8,128)S(1)}, f32[32,128]{1,0:T(8,128)}, u32[]{:S(2)}) copy-start(f32[32,128]{1,0:T(8,128)} %get-tuple-element.5) | copy-start | bytes 49156

commit v3 on v2

--- a/solution.py
+++ b/solution.py
@@ -148,7 +148,7 @@
     return (value + unit - 1) // unit * unit
 
 
-def whole_kernel(
+def ocean_kernel(
     sections,
     strips,
     levels,
@@ -161,11 +161,11 @@
     sea_ref,
     lists_ref,
     trac_ref,
-    out_c,
-    out_h,
+    received_ref,
     grid,
     halo_out,
     halo_in,
+    phyto_own,
     phyto_out,
     phyto_in,
     placed,
@@ -176,8 +176,11 @@
     fields,
     send,
     recv,
+    own_sem,
     halo_ssem,
     halo_rsem,
+    pass_ssem,
+    pass_rsem,
     phyto_ssem,
     phyto_rsem,
     rim_ssem,
@@ -186,7 +189,6 @@
     field_rsem,
 ):
     owners = (sections - 1) * strips
-    species = trac_ref.shape[0]
     padded_rows = grid.shape[1]
     sec = lax.axis_index("sec")
     strip = lax.axis_index("gx")
@@ -203,11 +205,23 @@
 
     @pl.when(sec == 0)
     def _():
-        out_c[...] = trac_ref[...]
-        out_h[...] = jnp.zeros_like(out_h)
+        received_ref[...] = jnp.zeros_like(received_ref)
 
     @pl.when(sec > 0)
     def _():
+        barrier = pltpu.get_barrier_semaphore()
+
+        def greet(i, carry):
+            t = lax.rem(me + i, owners)
+            pl.semaphore_signal(
+                barrier, inc=1, device_id=(1 + t // strips, lax.rem(t, strips)), device_id_type=MESH
+            )
+            return carry
+
+        lax.fori_loop(1, owners, greet, 0)
+        own_copy = pltpu.make_async_copy(trac_ref.at[1], phyto_own, own_sem)
+        own_copy.start()
+
         def channel(c, rows):
             count = rows.stop - rows.start
 
@@ -237,23 +251,14 @@
                 return sun_ref[rows, :]
             return sea_ref[rows, :].astype(jnp.float32)
 
-        for c in range(grid.shape[0]):
-            halo_out[0, c] = channel(c, slice(width - HALO, width))
-            halo_out[1, c] = channel(c, slice(0, HALO))
-
+        spans = halo_spans(levels)
+        for c, (at, count) in enumerate(spans):
+            halo_out[0, at : at + count, :] = channel(c, slice(width - count, width))
+            halo_out[1, at : at + count, :] = channel(c, slice(0, count))
+
+        own_copy.wait()
         for h in range(strips):
-            phyto_out[h] = trac_ref[1, h * levels : (h + 1) * levels, :]
-
-        barrier = pltpu.get_barrier_semaphore()
-
-        def greet(i, carry):
-            t = lax.rem(me + i, owners)
-            pl.semaphore_signal(
-                barrier, inc=1, device_id=(1 + t // strips, lax.rem(t, strips)), device_id_type=MESH
-            )
-            return carry
-
-        lax.fori_loop(1, owners, greet, 0)
+            phyto_out[h] = phyto_own[h * levels : (h + 1) * levels, :]
         pl.semaphore_wait(barrier, owners - 1)
 
         def edge_copy(out_ref, in_ref, ssem, rsem, side):
@@ -286,16 +291,17 @@
             return carry
 
         lax.fori_loop(1, owners, send_phyto, 0)
-        for copy in halo_copies:
-            copy.start()
+        alone = sec < 2
+        takes = [alone | (lax.rem(sec, 2) == side) for side in range(2)]
+        for copy, mine in zip(halo_copies, takes):
+            pl.when(mine)(copy.start)
 
         phyto_in[me] = phyto_out[strip]
 
         for c in range(grid.shape[0]):
-            if padded_rows > width + 2 * HALO:
-                grid[c, width + 2 * HALO :, :] = jnp.zeros(
-                    (padded_rows - width - 2 * HALO, lat), jnp.float32
-                )
+            grid[c, 0:HALO, :] = jnp.zeros((HALO, lat), jnp.float32)
+            tail = width // 8 * 8 + HALO
+            grid[c, tail:, :] = jnp.zeros((padded_rows - tail, lat), jnp.float32)
             grid[c, HALO : HALO + width, :] = channel(c, slice(0, width))
 
         def wait_phyto(i, carry):
@@ -349,11 +355,26 @@
         rim_copies = [edge_copy(rim_out, rim_in, rim_ssem, rim_rsem, side) for side in range(2)]
         for copy in rim_copies:
             copy.start()
-        for copy in halo_copies:
-            copy.wait()
-        for c in range(grid.shape[0]):
-            grid[c, 0:HALO, :] = halo_in[0, c]
-            grid[c, HALO + width : 2 * HALO + width, :] = halo_in[1, c]
+        for copy, mine in zip(halo_copies, takes):
+            pl.when(mine)(copy.wait)
+
+        @pl.when(jnp.logical_not(alone))
+        def _():
+            side = lax.rem(sec, 2)
+            hand_on = pltpu.make_async_remote_copy(
+                src_ref=halo_in.at[side],
+                dst_ref=halo_in.at[side],
+                send_sem=pass_ssem,
+                recv_sem=pass_rsem,
+                device_id=(sec + 1 - 2 * side, strip),
+                device_id_type=MESH,
+            )
+            hand_on.start()
+            hand_on.wait()
+
+        for c, (at, count) in enumerate(spans):
+            grid[c, HALO - count : HALO, :] = halo_in[0, at : at + count, :]
+            grid[c, HALO + width : HALO + width + count, :] = halo_in[1, at : at + count, :]
 
         lane = lax.broadcasted_iota(jnp.int32, (padded_rows, lat), 1)
         not_last = lane < lat - 1
@@ -486,6 +507,40 @@
 
             lax.fori_loop(1, strips, one, 0)
 
+        for step in range(STEPS):
+            ocean_step()
+            column_fields()
+            send_fields(step)
+            if step == 0:
+                for copy in rim_copies:
+                    copy.wait()
+                for k in range(levels):
+                    phyto_grid[k, HALO - 2 : HALO, :] = rim_in[0, 2 * k : 2 * k + 2, :]
+                    phyto_grid[k, HALO + width : HALO + width + 2, :] = rim_in[
+                        1, 2 * k : 2 * k + 2, :
+                    ]
+                weights = transport_weights([None] + [fields[k] for k in range(levels - 1)])
+                mixing = [None] + [fields[levels - 1 + k] for k in range(levels - 1)]
+                moved = transport([phyto_grid[k] for k in range(levels)], weights, mixing)
+                _, heats = light_profile(moved, grid[sun_row])
+                for k in range(levels):
+                    grid[first_heat + k] = heats[k]
+        for step in range(STEPS):
+            wait_fields(step)
+            received_ref[step] = recv[step]
+
+
+def tracer_kernel(strips, levels, recv, trac_ref, out_c, out_h):
+    species = trac_ref.shape[0]
+    sec = lax.axis_index("sec")
+
+    @pl.when(sec == 0)
+    def _():
+        out_c[...] = trac_ref[...]
+        out_h[...] = jnp.zeros_like(out_h)
+
+    @pl.when(sec > 0)
+    def _():
         def advance(step, source, last):
             def received(c):
                 return recv[step, pl.ds(c, strips, stride=ROWS_SENT), :]
@@ -545,27 +600,13 @@
                     out_c[n, level_rows(k), :] = jnp.where(valid, now[k] + DT_BIO * change, column[k])
 
         for step in range(STEPS):
-            ocean_step()
-            column_fields()
-            send_fields(step)
-            if step == 0:
-                for copy in rim_copies:
-                    copy.wait()
-                for k in range(levels):
-                    phyto_grid[k, HALO - 2 : HALO, :] = rim_in[0, 2 * k : 2 * k + 2, :]
-                    phyto_grid[k, HALO + width : HALO + width + 2, :] = rim_in[
-                        1, 2 * k : 2 * k + 2, :
-                    ]
-                weights = transport_weights([None] + [fields[k] for k in range(levels - 1)])
-                mixing = [None] + [fields[levels - 1 + k] for k in range(levels - 1)]
-                moved = transport([phyto_grid[k] for k in range(levels)], weights, mixing)
-                _, heats = light_profile(moved, grid[sun_row])
-                for k in range(levels):
-                    grid[first_heat + k] = heats[k]
-        wait_fields(0)
-        advance(0, trac_ref, False)
-        wait_fields(1)
-        advance(1, out_c, True)
+            advance(step, trac_ref if step == 0 else out_c, step == STEPS - 1)
+
+
+def halo_spans(levels):
+    counts = [7] * (2 * levels) + [6] * (2 * levels) + [5] * levels + [6, 6, 2, 6]
+    starts = np.cumsum([0] + counts)
+    return [(int(at), count) for at, count in zip(starts, counts)]
 
 
 def per_device(ocean_state, heat_first, wind_stress, shortwave, sea_mask, owner_cols, tracers):
@@ -580,18 +621,22 @@
     halves = lat // LANES
     f32 = jnp.float32
     vmem = pl.BlockSpec(memory_space=pltpu.VMEM)
-    new_c, new_h = pl.pallas_call(
-        functools.partial(whole_kernel, sections, strips, levels, width, lat),
-        out_shape=(
-            jax.ShapeDtypeStruct((species, strips * levels, LANES), f32),
-            jax.ShapeDtypeStruct((strips * levels, LANES), f32),
-        ),
-        in_specs=[vmem] * 7,
-        out_specs=(vmem, vmem),
+    halo_rows = ceil_to(sum(halo_spans(levels)[-1]), 8)
+    tracer_view = (
+        tracers.reshape(species, levels, strips, LANES)
+        .transpose(0, 2, 1, 3)
+        .reshape(species, strips * levels, LANES)
+    )
+    received = pl.pallas_call(
+        functools.partial(ocean_kernel, sections, strips, levels, width, lat),
+        out_shape=jax.ShapeDtypeStruct((STEPS, strips * ROWS_SENT, LANES), f32),
+        in_specs=[vmem] * 6 + [pl.BlockSpec(memory_space=pl.ANY)],
+        out_specs=vmem,
         scratch_shapes=[
             pltpu.VMEM((channels, padded_rows, lat), f32),
-            pltpu.VMEM((2, channels, HALO, lat), f32),
-            pltpu.VMEM((2, channels, HALO, lat), f32),
+            pltpu.VMEM((2, halo_rows, lat), f32),
+            pltpu.VMEM((2, halo_rows, lat), f32),
+            pltpu.VMEM((strips * levels, LANES), f32),
             pltpu.VMEM((strips, levels, LANES), f32),
             pltpu.VMEM((owners, levels, LANES), f32),
             pltpu.VMEM((3 * levels * place_rows, owners * LANES), jnp.bfloat16),
@@ -602,8 +647,11 @@
             pltpu.VMEM((2 * levels - 1, padded_rows, lat), f32),
             pltpu.VMEM((STEPS, strips, ROWS_SENT, LANES), f32),
             pltpu.VMEM((STEPS, strips * ROWS_SENT, LANES), f32),
+            pltpu.SemaphoreType.DMA,
             pltpu.SemaphoreType.DMA((2,)),
             pltpu.SemaphoreType.DMA((2,)),
+            pltpu.SemaphoreType.DMA,
+            pltpu.SemaphoreType.DMA,
             pltpu.SemaphoreType.DMA((owners,)),
             pltpu.SemaphoreType.DMA((owners,)),
             pltpu.SemaphoreType.DMA((2,)),
@@ -612,7 +660,9 @@
             pltpu.SemaphoreType.DMA((STEPS, strips)),
         ],
         compiler_params=pltpu.CompilerParams(
-            collective_id=0, has_side_effects=True, vmem_limit_bytes=56 << 20
+            collective_id=0,
+            has_side_effects=True,
+            vmem_limit_bytes=(16 if owners * width < 512 else 56) << 20,
         ),
     )(
         ocean_state.reshape(fields_count, levels, width, halves, LANES)
@@ -623,10 +673,18 @@
         shortwave,
         sea_mask,
         owner_cols.reshape(owners, LANES),
-        tracers.reshape(species, levels, strips, LANES)
-        .transpose(0, 2, 1, 3)
-        .reshape(species, strips * levels, LANES),
+        tracer_view,
     )
+    new_c, new_h = pl.pallas_call(
+        functools.partial(tracer_kernel, strips, levels),
+        out_shape=(
+            jax.ShapeDtypeStruct((species, strips * levels, LANES), f32),
+            jax.ShapeDtypeStruct((strips * levels, LANES), f32),
+        ),
+        in_specs=[vmem] * 2,
+        out_specs=(vmem, vmem),
+        compiler_params=pltpu.CompilerParams(vmem_limit_bytes=16 << 20),
+    )(received, tracer_view)
     new_c = new_c.reshape(species, strips, levels, LANES).transpose(0, 2, 1, 3)
     new_h = new_h.reshape(strips, levels, LANES).transpose(1, 0, 2)
     return new_c.reshape(tracers.shape), new_h.reshape(levels, -1)

time: 30.1 us -> 29.3 us (0.973); the launches traced: 29.9 us -> 28.8 us
  Pallas kernels: 27 us -> 22.6 us
  local copies, waits for them, and re-layouts: 2.32 us -> 5.57 us
    pallas_call x1 -> x2, Pallas kernels: 27 us -> 22.6 us  [the longest x1 21.4 us: per_device(): pl.pallas_call(functools.partial(ocean_kernel, sections, strips, levels,...]
    unnamed x4 -> x16, local copies, waits for them, and re-layouts: 2.32 us -> 5.57 us
where the time goes in v3:
time: 29.3 us; the launch traced here: 28.8 us
  Pallas kernels  22.6 us (77%)
  local copies, waits for them, and re-layouts  5.57 us (19%)
  between operations  0.66 us (2%)
    pallas_call x1, Pallas kernels, per_device(): pl.pallas_call(functools.partial(ocean_kernel, sections, strips, levels,...  21.4 us
    unnamed x16, local copies, waits for them, and re-layouts  5.57 us
    pallas_call x1, Pallas kernels, per_device(): pl.pallas_call(functools.partial(tracer_kernel, strips, levels), out_shap...  1.19 us

profile of v3, /device:TPU:1, one launch (start us, length us, event | category | flops | bytes accessed | tf_op | source)
XLA Modules:
  0.0 28.8 jit_solution(17477519672943253084)
XLA Ops:
  0.6 0.0 copy-start
  0.6 1.0 %copy-done = f32[19,4,1024]{2,1,0:T(4,128)S(1)} copy-done((f32[19,4,1024]{2,1,0:T(4,128)S(1)}, f32[19,4,1024]{2,1,0:T(4,128)}, u32[]{:S(2)}) %copy-start) | copy-done | bytes 311320
  1.6 0.0 copy-start.2
  1.6 0.9 %copy-done.2 = f32[4,4,12,256]{3,1,2,0:T(4,128)S(1)} copy-done((f32[4,4,12,256]{3,1,2,0:T(4,128)S(1)}, f32[4,4,12,256]{3,1,2,0:T(4,128)}, u32[]{:S(2)}) %copy-start.2) | copy-done | bytes 196632
  2.5 0.0 copy-start.3
  2.5 0.8 %copy-done.3 = f32[4,12,256]{2,0,1:T(4,128)S(1)} copy-done((f32[4,12,256]{2,0,1:T(4,128)S(1)}, f32[4,12,256]{2,0,1:T(4,128)}, u32[]{:S(2)}) %copy-start.3) | copy-done | bytes 49176
  3.3 0.0 copy-start.4
  3.3 0.7 %copy-done.4 = f32[2,12,256]{2,0,1:T(2,128)S(1)} copy-done((f32[2,12,256]{2,0,1:T(2,128)S(1)}, f32[2,12,256]{2,0,1:T(2,128)}, u32[]{:S(2)}) %copy-start.4) | copy-done | bytes 24600
  4.1 0.0 copy-start.5
  4.1 0.7 %copy-done.5 = f32[12,256]{1,0:T(8,128)S(1)} copy-done((f32[12,256]{1,0:T(8,128)S(1)}, f32[12,256]{1,0:T(8,128)}, u32[]{:S(2)}) %copy-start.5) | copy-done | bytes 12312
  4.8 0.0 copy-start.6
  4.8 0.7 %copy-done.6 = s32[12,256]{1,0:T(8,128)S(1)} copy-done((s32[12,256]{1,0:T(8,128)S(1)}, s32[12,256]{1,0:T(8,128)}, u32[]{:S(2)}) %copy-start.6) | copy-done | bytes 12312
  5.5 0.0 copy-start.7
  5.5 0.7 %copy-done.7 = s32[1,3,8,128]{3,2,1,0:T(8,128)S(1)} copy-done((s32[1,3,8,128]{3,2,1,0:T(8,128)S(1)}, s32[1,3,8,128]{3,2,1,0:T(8,128)}, u32[]{:S(2)}) %copy-start.7) | copy-done | bytes 12312
  6.2 0.0 copy-start.1
  6.2 21.4 %shard_map.86.recv = f32[2,128,128]{2,1,0:T(8,128)S(1)} custom-call(f32[384,128]{1,0:T(8,128)S(1)} %bitcast.33, f32[96,128]{1,0:T(8,128)S(1)} %bitcast.34, f32[48,128]{1,0:T(8,128)S(1)} %bitcast.35, f32[12,256]{1,0:T(8,128)S(1)} %copy-done.5, s32[12,256]{1,0:T(8,128)S(1)} %copy-done.6, s32[24,128]{1,0:T(8,128)S(1)} %bitcast.36, f32[19,32,128]{2,1,0:T(8,128)S(1)} %bitcast.31), custom_call_target="tpu_custom_call" | custom-call | tf_op jit(solution)/shard_map/pallas_call | solution.py:630
  27.6 0.0 copy-done.1
  27.6 1.2 %shard_map.87 = (f32[19,32,128]{2,1,0:T(8,128)}, f32[32,128]{1,0:T(8,128)}) custom-call(f32[2,128,128]{2,1,0:T(8,128)S(1)} %shard_map.86.recv, f32[19,32,128]{2,1,0:T(8,128)S(1)} %bitcast.32), custom_call_target="tpu_custom_call" | custom-call | tf_op jit(solution)/shard_map/pallas_call | solution.py:678
Async XLA Ops:
  0.6 1.0 %copy-start = (f32[19,4,1024]{2,1,0:T(4,128)S(1)}, f32[19,4,1024]{2,1,0:T(4,128)}, u32[]{:S(2)}) copy-start(f32[19,4,1024]{2,1,0:T(4,128)} %param.13) | copy-start | bytes 933892
  1.6 0.9 %copy-start.2 = (f32[4,4,12,256]{3,1,2,0:T(4,128)S(1)}, f32[4,4,12,256]{3,1,2,0:T(4,128)}, u32[]{:S(2)}) copy-start(f32[4,4,12,256]{3,1,2,0:T(4,128)} %param.7) | copy-start | bytes 589828
  2.5 0.8 %copy-start.3 = (f32[4,12,256]{2,0,1:T(4,128)S(1)}, f32[4,12,256]{2,0,1:T(4,128)}, u32[]{:S(2)}) copy-start(f32[4,12,256]{2,0,1:T(4,128)} %param.8) | copy-start | bytes 147460
  3.3 0.7 %copy-start.4 = (f32[2,12,256]{2,0,1:T(2,128)S(1)}, f32[2,12,256]{2,0,1:T(2,128)}, u32[]{:S(2)}) copy-start(f32[2,12,256]{2,0,1:T(2,128)} %param.9) | copy-start | bytes 73732
  4.1 0.7 %copy-start.5 = (f32[12,256]{1,0:T(8,128)S(1)}, f32[12,256]{1,0:T(8,128)}, u32[]{:S(2)}) copy-start(f32[12,256]{1,0:T(8,128)} %sun_ref.1) | copy-start | bytes 36868
  4.8 0.7 %copy-start.6 = (s32[12,256]{1,0:T(8,128)S(1)}, s32[12,256]{1,0:T(8,128)}, u32[]{:S(2)}) copy-start(s32[12,256]{1,0:T(8,128)} %sea_ref.1) | copy-start | bytes 36868
  5.5 0.7 %copy-start.7 = (s32[1,3,8,128]{3,2,1,0:T(8,128)S(1)}, s32[1,3,8,128]{3,2,1,0:T(8,128)}, u32[]{:S(2)}) copy-start(s32[1,3,8,128]{3,2,1,0:T(8,128)} %param.12) | copy-start | bytes 36868
  6.2 21.4 %copy-start.1 = (f32[19,4,1024]{2,1,0:T(4,128)S(1)}, f32[19,4,1024]{2,1,0:T(4,128)}, u32[]{:S(2)}) copy-start(f32[19,4,1024]{2,1,0:T(4,128)} %param.13) | copy-start | bytes 933892

commit v4 on v3

--- a/solution.py
+++ b/solution.py
@@ -662,7 +662,7 @@
         compiler_params=pltpu.CompilerParams(
             collective_id=0,
             has_side_effects=True,
-            vmem_limit_bytes=(16 if owners * width < 512 else 56) << 20,
+            vmem_limit_bytes=56 << 20,
         ),
     )(
         ocean_state.reshape(fields_count, levels, width, halves, LANES)

time: 29.3 us -> 25.8 us (0.88); the launches traced: 28.8 us -> 25.7 us
  local copies, waits for them, and re-layouts: 5.57 us -> 0.9 us
  Pallas kernels: 22.6 us -> 24.1 us
    unnamed x16 -> x4, local copies, waits for them, and re-layouts: 5.57 us -> 0.9 us
    pallas_call x1, Pallas kernels: 21.4 us -> 22.9 us  [per_device(): pl.pallas_call(functools.partial(ocean_kernel, sections, strips, levels,...]
where the time goes in v4:
time: 25.8 us; the launch traced here: 25.7 us
  Pallas kernels  24.1 us (93%)
  local copies, waits for them, and re-layouts  0.9 us (3%)
  between operations  0.66 us (3%)
    pallas_call x1, Pallas kernels, per_device(): pl.pallas_call(functools.partial(ocean_kernel, sections, strips, levels,...  22.9 us
    pallas_call x1, Pallas kernels, per_device(): pl.pallas_call(functools.partial(tracer_kernel, strips, levels), out_shap...  1.17 us
    unnamed x4, local copies, waits for them, and re-layouts  0.9 us

profile of v4, /device:TPU:1, one launch (start us, length us, event | category | flops | bytes accessed | tf_op | source)
XLA Modules:
  0.0 25.7 jit_solution(3262756216918375608)
XLA Ops:
  0.6 0.0 copy-start
  0.6 22.9 %shard_map.86.recv = f32[2,128,128]{2,1,0:T(8,128)} custom-call(f32[384,128]{1,0:T(8,128)} %bitcast.33, f32[96,128]{1,0:T(8,128)} %bitcast.34, f32[48,128]{1,0:T(8,128)} %bitcast.35, f32[12,256]{1,0:T(8,128)} %sun_ref.1, s32[12,256]{1,0:T(8,128)} %sea_ref.1, s32[24,128]{1,0:T(8,128)} %bitcast.36, f32[19,32,128]{2,1,0:T(8,128)} %bitcast.31), custom_call_target="tpu_custom_call" | custom-call | tf_op jit(solution)/shard_map/pallas_call | solution.py:630
  23.6 0.0 copy-done
  23.6 0.0 copy-start.1
  23.6 0.9 %copy-done.1 = f32[2,128,128]{2,1,0:T(8,128)S(1)} copy-done((f32[2,128,128]{2,1,0:T(8,128)S(1)}, f32[2,128,128]{2,1,0:T(8,128)}, u32[]{:S(2)}) %copy-start.1) | copy-done | bytes 131096
  24.5 1.2 %shard_map.87 = (f32[19,32,128]{2,1,0:T(8,128)}, f32[32,128]{1,0:T(8,128)}) custom-call(f32[2,128,128]{2,1,0:T(8,128)S(1)} %copy-done.1, f32[19,32,128]{2,1,0:T(8,128)S(1)} %bitcast.32), custom_call_target="tpu_custom_call" | custom-call | tf_op jit(solution)/shard_map/pallas_call | solution.py:678
Async XLA Ops:
  0.6 23.0 %copy-start = (f32[19,4,1024]{2,1,0:T(4,128)S(1)}, f32[19,4,1024]{2,1,0:T(4,128)}, u32[]{:S(2)}) copy-start(f32[19,4,1024]{2,1,0:T(4,128)} %param.13) | copy-start | bytes 933892
  23.6 0.9 %copy-start.1 = (f32[2,128,128]{2,1,0:T(8,128)S(1)}, f32[2,128,128]{2,1,0:T(8,128)}, u32[]{:S(2)}) copy-start(f32[2,128,128]{2,1,0:T(8,128)} %shard_map.86.recv) | copy-start | bytes 393220

commit v5 on v4

--- a/solution.py
+++ b/solution.py
@@ -290,11 +290,12 @@
             phyto_copy(lax.rem(me + i, owners), me).start()
             return carry
 
-        lax.fori_loop(1, owners, send_phyto, 0)
         alone = sec < 2
         takes = [alone | (lax.rem(sec, 2) == side) for side in range(2)]
         for copy, mine in zip(halo_copies, takes):
             pl.when(mine)(copy.start)
+
+        lax.fori_loop(1, owners, send_phyto, 0)
 
         phyto_in[me] = phyto_out[strip]
 

time: 25.8 us -> 27.3 us (1.058)
  the two profiles are of different devices: /device:TPU:1 before, /device:TPU:2 now
where the time goes in v5:
time: 27.3 us; the launch traced here: 27.1 us
  Pallas kernels  25.5 us (93%)
  local copies, waits for them, and re-layouts  0.9 us (3%)
  between operations  0.66 us (2%)
    pallas_call x1, Pallas kernels, per_device(): pl.pallas_call(functools.partial(ocean_kernel, sections, strips, levels,...  24.4 us
    pallas_call x1, Pallas kernels, per_device(): pl.pallas_call(functools.partial(tracer_kernel, strips, levels), out_shap...  1.17 us
    unnamed x4, local copies, waits for them, and re-layouts  0.9 us

profile of v5, /device:TPU:2, one launch (start us, length us, event | category | flops | bytes accessed | tf_op | source)
XLA Modules:
  0.0 27.1 jit_solution(7980380591077479865)
XLA Ops:
  0.6 0.0 copy-start
  0.6 24.4 %shard_map.86.recv = f32[2,128,128]{2,1,0:T(8,128)} custom-call(f32[384,128]{1,0:T(8,128)} %bitcast.33, f32[96,128]{1,0:T(8,128)} %bitcast.34, f32[48,128]{1,0:T(8,128)} %bitcast.35, f32[12,256]{1,0:T(8,128)} %sun_ref.1, s32[12,256]{1,0:T(8,128)} %sea_ref.1, s32[24,128]{1,0:T(8,128)} %bitcast.36, f32[19,32,128]{2,1,0:T(8,128)} %bitcast.31), custom_call_target="tpu_custom_call" | custom-call | tf_op jit(solution)/shard_map/pallas_call | solution.py:631
  25.0 0.0 copy-done
  25.0 0.0 copy-start.1
  25.0 0.9 %copy-done.1 = f32[2,128,128]{2,1,0:T(8,128)S(1)} copy-done((f32[2,128,128]{2,1,0:T(8,128)S(1)}, f32[2,128,128]{2,1,0:T(8,128)}, u32[]{:S(2)}) %copy-start.1) | copy-done | bytes 131096
  25.9 1.2 %shard_map.87 = (f32[19,32,128]{2,1,0:T(8,128)}, f32[32,128]{1,0:T(8,128)}) custom-call(f32[2,128,128]{2,1,0:T(8,128)S(1)} %copy-done.1, f32[19,32,128]{2,1,0:T(8,128)S(1)} %bitcast.32), custom_call_target="tpu_custom_call" | custom-call | tf_op jit(solution)/shard_map/pallas_call | solution.py:679
Async XLA Ops:
  0.6 24.4 %copy-start = (f32[19,4,1024]{2,1,0:T(4,128)S(1)}, f32[19,4,1024]{2,1,0:T(4,128)}, u32[]{:S(2)}) copy-start(f32[19,4,1024]{2,1,0:T(4,128)} %param.13) | copy-start | bytes 933892
  25.0 0.9 %copy-start.1 = (f32[2,128,128]{2,1,0:T(8,128)S(1)}, f32[2,128,128]{2,1,0:T(8,128)}, u32[]{:S(2)}) copy-start(f32[2,128,128]{2,1,0:T(8,128)} %shard_map.86.recv) | copy-start | bytes 393220
